TPU v7x, 32 devices: a whole 2x2x4 slice. The times are simulated.
32 devices in a mesh: sub: 8 (over y, x, core), grp: 4 (over z).
Axes of the slice: x: 2, y: 2, z: 4, core: 2. Of those that a mesh axis runs over, the one named last changes fastest.
Arguments:
- node_rows: bfloat16 [32768, 512], P(('sub', 'grp')), may hold values from -6 to 6
- owners: int32 [32768], P(('sub', 'grp')), may hold values from 0 to 31, as said below
- tile_src: int32 [8, 4, 16, 2], P('sub', 'grp'), may hold values from 0 to 15
- neighbors: int32 [8, 4, 2048, 16], P('sub', 'grp'), may hold values from 0 to 127
- pool_pair: int32 [8, 4, 2048], P('sub', 'grp'), may hold values from 0 to 2047, each once within a row
- pool_quad: int32 [4, 4, 2048], P(None, 'grp'), may hold values from 0 to 2047, each once within a row
- pool_top: int32 [2, 4, 2048], P(None, 'grp'), may hold values from 0 to 2047, each once within a row
- edge_in: bfloat16 [2, 512, 512], replicated, may hold values from -0.25 to 0.25
- edge_bias: float32 [512], replicated, may hold values from -4 to 4
- edge_out: bfloat16 [512, 512], replicated, may hold values from -0.25 to 0.25
- node_in: bfloat16 [2, 512, 512], replicated, may hold values from -0.25 to 0.25
- node_bias: float32 [512], replicated, may hold values from -4 to 4
- node_out: bfloat16 [512, 512], replicated, may hold values from -0.25 to 0.25
- out_gain: float32 [512], replicated, may hold values from 0.1 to 1.9
- coarse: bfloat16 [3, 512, 512], replicated, may hold values from -0.25 to 0.25
Outputs:
- updated: bfloat16 [65536, 512], P(('sub', 'grp'))
Inputs may be any that keep to these rules, and one draw needn't show every extreme that they name: `owners`: at most 64 nodes of one shard go to one owner, and one owner receives exactly 64 nodes from every shard. `pool_pair`: every row of the pooling map is a permutation of the 2048 slots. `pool_quad`: every row of the pooling map is a permutation of the 2048 slots. `pool_top`: every row of the pooling map is a permutation of the 2048 slots.
All inputs are finite; a program needn't handle non-finite values.
Results may differ from a plain program's by a relative error of at most 0.007.
Values may be sent and summed in bfloat16 or wider, within the bound.
A program may use at most 64 MiB of HBM per device.

v0:
```python
import math

import jax
import jax.numpy as jnp
from jax import lax
from jax.sharding import PartitionSpec as P

BLK = 128
TPB = 2
NBR = 8


epsilon = 1e-05


def swapped(shard, axis, apart):
    return lax.ppermute(shard, axis, [(i, i ^ 1 << apart) for i in range(lax.axis_size(axis))])


def block_sum(proj_dst, proj_src, present, tile_rows, near_rows, block_index):
    start = block_index * BLK
    dst_rows = lax.dynamic_slice_in_dim(proj_dst, start, BLK, 0).astype(jnp.float32)
    near_block = lax.dynamic_slice_in_dim(near_rows, start, BLK, 0)
    features = proj_src.shape[1]
    column_ids = jnp.arange(BLK, dtype=jnp.int32)
    total = jnp.zeros((BLK, features), jnp.float32)
    for tile in range(TPB):
        src_start = tile_rows[block_index, tile] * BLK
        src_rows = lax.dynamic_slice_in_dim(proj_src, src_start, BLK, 0)
        src_marks = lax.dynamic_slice_in_dim(present, src_start, BLK, 0)
        picks = near_block[:, tile * NBR : (tile + 1) * NBR].reshape(BLK * NBR)
        selector = picks[:, None] == column_ids[None, :]
        gathered = jnp.dot(
            selector.astype(jnp.bfloat16), src_rows, preferred_element_type=jnp.float32
        ).reshape(BLK, NBR, features)
        weight = jnp.sum(jnp.where(selector, src_marks[None, :], 0.0), axis=1).reshape(BLK, NBR)
        total = total + jnp.sum(
            jax.nn.silu(dst_rows[:, None, :] + gathered) * weight[:, :, None], axis=1
        )
    return total


def refine(total, count, weight):
    mean_rows = total / jnp.maximum(count, 1.0)[:, None]
    rounded = mean_rows.astype(jnp.bfloat16)
    lifted = jnp.dot(rounded, weight, preferred_element_type=jnp.float32)
    return (mean_rows + jax.nn.silu(lifted)).astype(jnp.bfloat16)


def invert(perm):
    return jnp.zeros(perm.shape, jnp.int32).at[perm].set(jnp.arange(perm.shape[0], dtype=jnp.int32))


def weighted(values, counts):
    return counts[:, None] * values.astype(jnp.float32)


def body(
    node_rows,
    owners,
    tile_src,
    neighbors,
    pool_pair,
    pool_quad,
    pool_top,
    edge_in,
    edge_bias,
    edge_out,
    node_in,
    node_bias,
    node_out,
    out_gain,
    coarse,
):
    wide_count = lax.axis_size("sub")
    narrow_count = lax.axis_size("grp")
    owner_count = wide_count * narrow_count
    slot_rows = neighbors.shape[2]
    features = node_rows.shape[1]
    capacity = slot_rows // owner_count
    matches = (owners[:, None] == jnp.arange(owner_count, dtype=jnp.int32)[None, :]).astype(
        jnp.int32
    )
    position = jnp.sum((jnp.cumsum(matches, axis=0) - matches) * matches, axis=1)
    target = owners * capacity + position
    placing = jnp.arange(slot_rows, dtype=jnp.int32)[:, None] == target[None, :]
    outgoing = jnp.dot(
        placing.astype(jnp.bfloat16), node_rows, preferred_element_type=jnp.float32
    ).astype(jnp.bfloat16)
    filled = jnp.sum(placing.astype(jnp.float32), axis=1).astype(jnp.bfloat16)
    arrived, marked = (
        lax.all_to_all(
            outgoing.reshape(owner_count, capacity, features),
            ("sub", "grp"),
            split_axis=0,
            concat_axis=0,
            tiled=True,
        ),
        lax.all_to_all(
            filled.reshape(owner_count, capacity),
            ("sub", "grp"),
            split_axis=0,
            concat_axis=0,
            tiled=True,
        ),
    )
    slots = arrived.reshape(slot_rows, features)
    present = marked.reshape(slot_rows).astype(jnp.float32)
    proj_dst = (jnp.dot(slots, edge_in[0], preferred_element_type=jnp.float32) + edge_bias).astype(
        jnp.bfloat16
    )
    proj_src = jnp.dot(slots, edge_in[1], preferred_element_type=jnp.float32).astype(jnp.bfloat16)
    block_total = slot_rows // BLK
    group_size = math.gcd(4, block_total)
    tile_rows = tile_src[0, 0]
    near_rows = neighbors[0, 0]

    def one_group(first):
        return jax.vmap(
            lambda offset: block_sum(
                proj_dst, proj_src, present, tile_rows, near_rows, first * group_size + offset
            )
        )(jnp.arange(group_size, dtype=jnp.int32))

    summed = lax.map(one_group, jnp.arange(block_total // group_size, dtype=jnp.int32))
    agg = summed.reshape(slot_rows, features).astype(jnp.bfloat16)
    message = jnp.dot(agg, edge_out, preferred_element_type=jnp.float32).astype(jnp.bfloat16)
    hidden = jax.nn.silu(
        jnp.dot(slots, node_in[0], preferred_element_type=jnp.float32)
        + jnp.dot(message, node_in[1], preferred_element_type=jnp.float32)
        + node_bias
    ).astype(jnp.bfloat16)
    delta = jnp.dot(hidden, node_out, preferred_element_type=jnp.float32)
    normed = delta * lax.rsqrt(jnp.mean(delta * delta, axis=-1, keepdims=True) + epsilon)
    fine = (present[:, None] * (slots.astype(jnp.float32) + out_gain * normed)).astype(jnp.bfloat16)
    perm_pair = pool_pair[0, 0]
    side_rows = fine[perm_pair]
    side_counts = present[perm_pair]
    other_rows, other_counts = swapped((side_rows, side_counts.astype(jnp.bfloat16)), "sub", 0)
    other_counts = other_counts.astype(jnp.float32)
    count_one = side_counts + other_counts
    level_one = refine(
        weighted(side_rows, side_counts) + weighted(other_rows, other_counts), count_one, coarse[0]
    )
    perm_quad = lax.dynamic_index_in_dim(pool_quad, lax.axis_index("sub") // 2, 0, keepdims=False)[
        0
    ]
    side_rows = level_one[perm_quad]
    side_counts = count_one[perm_quad]
    other_rows, other_counts = swapped((side_rows, side_counts.astype(jnp.bfloat16)), "sub", 1)
    other_counts = other_counts.astype(jnp.float32)
    count_two = side_counts + other_counts
    level_two = refine(
        weighted(side_rows, side_counts) + weighted(other_rows, other_counts), count_two, coarse[1]
    )
    perm_top = lax.dynamic_index_in_dim(pool_top, lax.axis_index("sub") // 4, 0, keepdims=False)[0]
    side_rows = level_two[perm_top]
    side_counts = count_two[perm_top]
    all_rows, all_counts = (
        lax.all_gather(side_rows, "grp", axis=0, tiled=True),
        lax.all_gather(side_counts.astype(jnp.bfloat16), "grp", axis=0, tiled=True),
    )
    all_rows = all_rows.reshape(narrow_count, slot_rows, features)
    all_counts = all_counts.reshape(narrow_count, slot_rows).astype(jnp.float32)
    total_three = jnp.sum(all_counts[:, :, None] * all_rows.astype(jnp.float32), axis=0)
    level_three = refine(total_three, jnp.sum(all_counts, axis=0), coarse[2])
    back_two = (
        level_two.astype(jnp.float32) + level_three[invert(perm_top)].astype(jnp.float32)
    ).astype(jnp.bfloat16)
    back_one = (
        level_one.astype(jnp.float32) + back_two[invert(perm_quad)].astype(jnp.float32)
    ).astype(jnp.bfloat16)
    updated = present[:, None] * (
        fine.astype(jnp.float32) + back_one[invert(perm_pair)].astype(jnp.float32)
    )
    return updated.astype(jnp.bfloat16)


def solution(mesh):
    in_specs = (
        P(("sub", "grp"), None),
        P(("sub", "grp")),
        P("sub", "grp", None, None),
        P("sub", "grp", None, None),
        P("sub", "grp", None),
        P(None, "grp", None),
        P(None, "grp", None),
        P(),
        P(),
        P(),
        P(),
        P(),
        P(),
        P(),
        P(),
    )
    out_specs = P(("sub", "grp"), None)
    return jax.shard_map(body, mesh=mesh, in_specs=in_specs, out_specs=out_specs, check_vma=False)
```

profile of v0, /device:TPU:0, one launch (start us, length us, event | category | flops | bytes accessed | tf_op | source)
XLA Modules:
  0.0 727.4 jit_solution(9957699891774394735)
XLA Ops:
  7.3 9.0 %reduce-window.6 = s32[32,8,128]{2,1,0:T(8,128)S(1)} reduce-window(s32[32,8,128]{2,1,0:T(8,128)S(1)} %fusion.50, s32[]{:T(128)} %constant.77.clone.1), window={size=1x1x128 pad=0_0x0_0x127_0}, to_apply=%region_0.0 | reduce-window | flops 4161536 | bytes 262148 | tf_op jit(solution)/shard_map/reduce-window
  38.6 45.9 %all-to-all-done.1 = bf16[32,64,512]{2,1,0:T(8,128)(2,1)S(1)} async-done(((bf16[32,64,512]{2,1,0:T(8,128)(2,1)}), bf16[32,64,512]{2,1,0:T(8,128)(2,1)S(1)}, u32[]{:S(2)}, u32[]{:S(2)}) %all-to-all-start.1) | async-done | bytes 2097184 | tf_op jit(solution)/shard_map/all_to_all | solution.py:92
  93.6 282.6 %while.28 = (s32[]{:T(128)}, bf16[4,4,128,512]{3,2,1,0:T(8,128)(2,1)}, s32[4]{0:T(128)S(1)}, bf16[2048,512]{1,0:T(8,128)(2,1)}, s32[2048,16]{0,1:T(8,128)}, /*in...) while((s32[]{:T(128)}, ...), condition=%wide.region_9.10_spmd, body=%wide.region_4.9_spmd.sunk | while | flops 1107288064 | bytes 14841849 | solution.py:125
  110.4 8.5 %while.34 = (s32[]{:T(128)}, bf16[2048,512]{1,0:T(8,128)(2,1)}, s32[4,2]{0,1:T(2,128)S(1)}, bf16[4,128,512]{2,1,0:T(8,128)(2,1)S(1)}, s32[]{:T(128)}) while((s32[]{:T(128)}, bf16[2048,512]{1,0:T(8,128)(2,1)}, s32[4,2]{0,1:T(2,128)S(1)}, bf16[4,128,512]{2,1,0:T(8,128)(2,1)S(1)}, s32[]{:T(128)}) %tuple.133), condition=%wide.while_cond.4, body=%wide.while_body.4.sunk | while | flops 2 | bytes 262241 | solution.py:29
  119.8 8.9 %while.31 = (s32[]{:T(128)}, bf16[2048,512]{1,0:T(8,128)(2,1)}, s32[4,2]{0,1:T(2,128)S(1)}, bf16[4,128,512]{2,1,0:T(8,128)(2,1)S(1)}, s32[]{:T(128)}) while((s32[]{:T(128)}, bf16[2048,512]{1,0:T(8,128)(2,1)}, s32[4,2]{0,1:T(2,128)S(1)}, bf16[4,128,512]{2,1,0:T(8,128)(2,1)S(1)}, s32[]{:T(128)}) %tuple.144), condition=%wide.while_cond, body=%wide.while_body.sunk | while | flops 2 | bytes 262241 | solution.py:22
  142.5 8.5 %while.32 = (s32[]{:T(128)}, bf16[2048,512]{1,0:T(8,128)(2,1)}, s32[4,2]{0,1:T(2,128)S(1)}, bf16[4,128,512]{2,1,0:T(8,128)(2,1)S(1)}, s32[]{:T(128)}) while((s32[]{:T(128)}, bf16[2048,512]{1,0:T(8,128)(2,1)}, s32[4,2]{0,1:T(2,128)S(1)}, bf16[4,128,512]{2,1,0:T(8,128)(2,1)S(1)}, s32[]{:T(128)}) %tuple.143), condition=%wide.while_cond.2, body=%wide.while_body.2.sunk | while | flops 2 | bytes 262241 | solution.py:29
  151.0 12.3 %multiply_reduce_fusion.5 = f32[4,128,512]{2,1,0:T(8,128)S(1)} fusion(f32[4,128,8]{2,1,0:T(8,128)S(1)} %mul.292, f32[4,128,512]{2,1,0:T(8,128)S(1)} %convert_element_type.279, bf16[4,128,512]{2,1,0:T(8,128)(2,1)S(1)} %get-tuple-element.410, s32[4,1024]{1,0:T(4,128)S(1)} %eq.161), kind=kOutput, calls=%fused_computation.29.clone.1 | convolution fusion | flops 551813120 | bytes 2654208 | tf_op jit(solution)/shard_map/while/body/eval_jaxpr/vmap()/dot_general | solution.py:33
  181.0 8.5 %while.34 = (s32[]{:T(128)}, bf16[2048,512]{1,0:T(8,128)(2,1)}, s32[4,2]{0,1:T(2,128)S(1)}, bf16[4,128,512]{2,1,0:T(8,128)(2,1)S(1)}, s32[]{:T(128)}) while((s32[]{:T(128)}, bf16[2048,512]{1,0:T(8,128)(2,1)}, s32[4,2]{0,1:T(2,128)S(1)}, bf16[4,128,512]{2,1,0:T(8,128)(2,1)S(1)}, s32[]{:T(128)}) %tuple.133), condition=%wide.while_cond.4, body=%wide.while_body.4.sunk | while | flops 2 | bytes 262241 | solution.py:29
  190.4 8.9 %while.31 = (s32[]{:T(128)}, bf16[2048,512]{1,0:T(8,128)(2,1)}, s32[4,2]{0,1:T(2,128)S(1)}, bf16[4,128,512]{2,1,0:T(8,128)(2,1)S(1)}, s32[]{:T(128)}) while((s32[]{:T(128)}, bf16[2048,512]{1,0:T(8,128)(2,1)}, s32[4,2]{0,1:T(2,128)S(1)}, bf16[4,128,512]{2,1,0:T(8,128)(2,1)S(1)}, s32[]{:T(128)}) %tuple.144), condition=%wide.while_cond, body=%wide.while_body.sunk | while | flops 2 | bytes 262241 | solution.py:22
  213.1 8.5 %while.32 = (s32[]{:T(128)}, bf16[2048,512]{1,0:T(8,128)(2,1)}, s32[4,2]{0,1:T(2,128)S(1)}, bf16[4,128,512]{2,1,0:T(8,128)(2,1)S(1)}, s32[]{:T(128)}) while((s32[]{:T(128)}, bf16[2048,512]{1,0:T(8,128)(2,1)}, s32[4,2]{0,1:T(2,128)S(1)}, bf16[4,128,512]{2,1,0:T(8,128)(2,1)S(1)}, s32[]{:T(128)}) %tuple.143), condition=%wide.while_cond.2, body=%wide.while_body.2.sunk | while | flops 2 | bytes 262241 | solution.py:29
  221.6 12.3 %multiply_reduce_fusion.5 = f32[4,128,512]{2,1,0:T(8,128)S(1)} fusion(f32[4,128,8]{2,1,0:T(8,128)S(1)} %mul.292, f32[4,128,512]{2,1,0:T(8,128)S(1)} %convert_element_type.279, bf16[4,128,512]{2,1,0:T(8,128)(2,1)S(1)} %get-tuple-element.410, s32[4,1024]{1,0:T(4,128)S(1)} %eq.161), kind=kOutput, calls=%fused_computation.29.clone.1 | convolution fusion | flops 551813120 | bytes 2654208 | tf_op jit(solution)/shard_map/while/body/eval_jaxpr/vmap()/dot_general | solution.py:33
  251.7 8.5 %while.34 = (s32[]{:T(128)}, bf16[2048,512]{1,0:T(8,128)(2,1)}, s32[4,2]{0,1:T(2,128)S(1)}, bf16[4,128,512]{2,1,0:T(8,128)(2,1)S(1)}, s32[]{:T(128)}) while((s32[]{:T(128)}, bf16[2048,512]{1,0:T(8,128)(2,1)}, s32[4,2]{0,1:T(2,128)S(1)}, bf16[4,128,512]{2,1,0:T(8,128)(2,1)S(1)}, s32[]{:T(128)}) %tuple.133), condition=%wide.while_cond.4, body=%wide.while_body.4.sunk | while | flops 2 | bytes 262241 | solution.py:29
  261.1 8.9 %while.31 = (s32[]{:T(128)}, bf16[2048,512]{1,0:T(8,128)(2,1)}, s32[4,2]{0,1:T(2,128)S(1)}, bf16[4,128,512]{2,1,0:T(8,128)(2,1)S(1)}, s32[]{:T(128)}) while((s32[]{:T(128)}, bf16[2048,512]{1,0:T(8,128)(2,1)}, s32[4,2]{0,1:T(2,128)S(1)}, bf16[4,128,512]{2,1,0:T(8,128)(2,1)S(1)}, s32[]{:T(128)}) %tuple.144), condition=%wide.while_cond, body=%wide.while_body.sunk | while | flops 2 | bytes 262241 | solution.py:22
  283.8 8.5 %while.32 = (s32[]{:T(128)}, bf16[2048,512]{1,0:T(8,128)(2,1)}, s32[4,2]{0,1:T(2,128)S(1)}, bf16[4,128,512]{2,1,0:T(8,128)(2,1)S(1)}, s32[]{:T(128)}) while((s32[]{:T(128)}, bf16[2048,512]{1,0:T(8,128)(2,1)}, s32[4,2]{0,1:T(2,128)S(1)}, bf16[4,128,512]{2,1,0:T(8,128)(2,1)S(1)}, s32[]{:T(128)}) %tuple.143), condition=%wide.while_cond.2, body=%wide.while_body.2.sunk | while | flops 2 | bytes 262241 | solution.py:29
  292.3 12.3 %multiply_reduce_fusion.5 = f32[4,128,512]{2,1,0:T(8,128)S(1)} fusion(f32[4,128,8]{2,1,0:T(8,128)S(1)} %mul.292, f32[4,128,512]{2,1,0:T(8,128)S(1)} %convert_element_type.279, bf16[4,128,512]{2,1,0:T(8,128)(2,1)S(1)} %get-tuple-element.410, s32[4,1024]{1,0:T(4,128)S(1)} %eq.161), kind=kOutput, calls=%fused_computation.29.clone.1 | convolution fusion | flops 551813120 | bytes 2654208 | tf_op jit(solution)/shard_map/while/body/eval_jaxpr/vmap()/dot_general | solution.py:33
  322.3 8.5 %while.34 = (s32[]{:T(128)}, bf16[2048,512]{1,0:T(8,128)(2,1)}, s32[4,2]{0,1:T(2,128)S(1)}, bf16[4,128,512]{2,1,0:T(8,128)(2,1)S(1)}, s32[]{:T(128)}) while((s32[]{:T(128)}, bf16[2048,512]{1,0:T(8,128)(2,1)}, s32[4,2]{0,1:T(2,128)S(1)}, bf16[4,128,512]{2,1,0:T(8,128)(2,1)S(1)}, s32[]{:T(128)}) %tuple.133), condition=%wide.while_cond.4, body=%wide.while_body.4.sunk | while | flops 2 | bytes 262241 | solution.py:29
  331.7 8.9 %while.31 = (s32[]{:T(128)}, bf16[2048,512]{1,0:T(8,128)(2,1)}, s32[4,2]{0,1:T(2,128)S(1)}, bf16[4,128,512]{2,1,0:T(8,128)(2,1)S(1)}, s32[]{:T(128)}) while((s32[]{:T(128)}, bf16[2048,512]{1,0:T(8,128)(2,1)}, s32[4,2]{0,1:T(2,128)S(1)}, bf16[4,128,512]{2,1,0:T(8,128)(2,1)S(1)}, s32[]{:T(128)}) %tuple.144), condition=%wide.while_cond, body=%wide.while_body.sunk | while | flops 2 | bytes 262241 | solution.py:22
  354.4 8.5 %while.32 = (s32[]{:T(128)}, bf16[2048,512]{1,0:T(8,128)(2,1)}, s32[4,2]{0,1:T(2,128)S(1)}, bf16[4,128,512]{2,1,0:T(8,128)(2,1)S(1)}, s32[]{:T(128)}) while((s32[]{:T(128)}, bf16[2048,512]{1,0:T(8,128)(2,1)}, s32[4,2]{0,1:T(2,128)S(1)}, bf16[4,128,512]{2,1,0:T(8,128)(2,1)S(1)}, s32[]{:T(128)}) %tuple.143), condition=%wide.while_cond.2, body=%wide.while_body.2.sunk | while | flops 2 | bytes 262241 | solution.py:29
  363.0 12.3 %multiply_reduce_fusion.5 = f32[4,128,512]{2,1,0:T(8,128)S(1)} fusion(f32[4,128,8]{2,1,0:T(8,128)S(1)} %mul.292, f32[4,128,512]{2,1,0:T(8,128)S(1)} %convert_element_type.279, bf16[4,128,512]{2,1,0:T(8,128)(2,1)S(1)} %get-tuple-element.410, s32[4,1024]{1,0:T(4,128)S(1)} %eq.161), kind=kOutput, calls=%fused_computation.29.clone.1 | convolution fusion | flops 551813120 | bytes 2654208 | tf_op jit(solution)/shard_map/while/body/eval_jaxpr/vmap()/dot_general | solution.py:33
  400.8 9.2 %gather_fusion.3 = bf16[2048,512]{1,0:T(8,128)(2,1)} fusion(bf16[2048,512]{1,0:T(8,128)(2,1)S(1)} %copy.43, s32[2048]{0:T(1024)S(1)} %copy-done.8), kind=kCustom, calls=%fused_computation.3 | custom fusion | bytes 4202496 | tf_op jit(solution)/shard_map/gather | solution.py:137
  411.7 11.8 %gather_fusion.2 = f32[2048]{0:T(1024)S(1)} fusion(f32[2048]{0:T(1024)S(1)} %get-tuple-element.602, s32[2048]{0:T(1024)S(1)} %copy-done.8), kind=kCustom, calls=%fused_computation.2 | custom fusion | bytes 24576 | tf_op jit(solution)/shard_map/gather | solution.py:138
  433.2 9.2 %gather_fusion.5 = bf16[2048,512]{1,0:T(8,128)(2,1)} fusion(bf16[2048,512]{1,0:T(8,128)(2,1)S(1)} %add_convert_fusion.4, s32[2048]{0:T(1024)S(1)} %broadcast_clamp_fusion.1), kind=kCustom, calls=%fused_computation.5 | custom fusion | bytes 4202496 | tf_op jit(solution)/shard_map/gather | solution.py:148
  444.5 11.8 %gather_fusion.4 = f32[2048]{0:T(1024)S(1)} fusion(f32[2048]{0:T(1024)S(1)} %get-tuple-element.163, s32[2048]{0:T(1024)S(1)} %broadcast_clamp_fusion.1), kind=kCustom, calls=%fused_computation.4 | custom fusion | bytes 24576 | tf_op jit(solution)/shard_map/gather | solution.py:149
  456.4 34.4 %collective-permute-done.2 = bf16[2048]{0:T(1024)(128)(2,1)S(1)} collective-permute-done((bf16[2048]{0:T(1024)(128)(2,1)S(1)}, bf16[2048]{0:T(1024)(128)(2,1)S(1)}, u32[]{:S(2)}, u32[]{:S(2)}) %collective-permute-start.2) | collective-permute-done | bytes 4128 | tf_op jit(solution)/shard_map/ppermute | solution.py:17
  498.5 11.1 %gather_fusion.7 = bf16[2048,512]{1,0:T(8,128)(2,1)} fusion(bf16[2048,512]{1,0:T(8,128)(2,1)} %add_convert_fusion.3, s32[2048]{0:T(1024)S(1)} %broadcast_clamp_fusion), kind=kCustom, calls=%fused_computation.7 | custom fusion | bytes 4202496 | tf_op jit(solution)/shard_map/gather | solution.py:157
  509.6 8.3 %scatter_custom_fusion = s32[2048]{0:T(1024)S(1)} fusion(s32[2048]{0:T(1024)S(1)} %bitcast.163, s32[2048]{0:T(1024)S(1)} %iota.34, s32[]{:T(128)} %constant.77.clone.1), kind=kCustom, calls=%fused_computation.123 | custom fusion | bytes 8196 | tf_op jit(solution)/shard_map/scatter | solution.py:51
  534.2 13.1 %gather_fusion.6 = bf16[2048]{0:T(1024)(128)(2,1)S(1)} fusion(bf16[2048]{0:T(1024)(128)(2,1)S(1)} %get-tuple-element.161, s32[2048]{0:T(1024)S(1)} %broadcast_clamp_fusion), kind=kCustom, calls=%fused_computation.6 | custom fusion | bytes 16384 | tf_op jit(solution)/shard_map/gather | solution.py:158
  547.3 15.1 %all_gather.6 = bf16[8192]{0:T(1024)(128)(2,1)S(1)} all-gather(bf16[2048]{0:T(1024)(128)(2,1)S(1)} %gather_fusion.6), channel_id=1, replica_groups=mesh['sub'=8,'grp'=4] {'grp'}, dimensions={0}, use_global_device_ids=true | all-gather | bytes 20480 | tf_op jit(solution)/shard_map/all_gather | solution.py:161
  562.5 95.6 %all-gather.3.cloned.1.call-done = bf16[8192,512]{1,0:T(8,128)(2,1)} async-done(((bf16[2048,512]{1,0:T(8,128)(2,1)}), bf16[8192,512]{1,0:T(8,128)(2,1)}) %all-gather.3.cloned.1.call-update) | async-done | bytes 8388624 | tf_op jit(solution)/shard_map/all_gather | solution.py:160
  667.9 11.1 %gather_fusion.8 = bf16[2048,512]{1,0:T(8,128)(2,1)} fusion(bf16[2048,512]{1,0:T(8,128)(2,1)} %add_convert_fusion.2, s32[2048]{0:T(1024)S(1)} %fusion.51), kind=kCustom, calls=%fused_computation.8 | custom fusion | bytes 4202496 | tf_op jit(solution)/shard_map/gather | solution.py:168
  683.1 11.1 %gather_fusion.9 = bf16[2048,512]{1,0:T(8,128)(2,1)} fusion(bf16[2048,512]{1,0:T(8,128)(2,1)} %add_convert_fusion.1, s32[2048]{0:T(1024)S(1)} %fusion.52), kind=kCustom, calls=%fused_computation.9 | custom fusion | bytes 4202496 | tf_op jit(solution)/shard_map/gather | solution.py:171
  697.7 11.1 %gather_fusion.10 = bf16[2048,512]{1,0:T(8,128)(2,1)} fusion(bf16[2048,512]{1,0:T(8,128)(2,1)} %add_convert_fusion, s32[2048]{0:T(1024)S(1)} %fusion.53), kind=kCustom, calls=%fused_computation.10 | custom fusion | bytes 4202496 | tf_op jit(solution)/shard_map/gather | solution.py:174
  (523 shorter events, 424.6 us)
Async XLA Ops:
  6.5 20.6 %copy-start = (bf16[1024,512]{1,0:T(8,128)(2,1)S(1)}, bf16[1024,512]{1,0:T(8,128)(2,1)}, u32[]{:S(2)}) copy-start(bf16[1024,512]{1,0:T(8,128)(2,1)} %param.17) | copy-start | bytes 3145732
  19.8 14.5 %all-to-all-start = ((bf16[32,1,64]{2,1,0:T(2,128)(2,1)}), bf16[32,1,64]{2,1,0:T(2,128)(2,1)S(1)}, u32[]{:S(2)}, u32[]{:S(2)}) async-start(bf16[32,1,64]{2,1,0:T(2,128)(2,1)} %convert_element_type.206), calls=%async_computation | async-start | bytes 32768 | tf_op jit(solution)/shard_map/all_to_all | solution.py:99
  30.8 6.5 copy-start.10
  34.3 50.2 %all-to-all-start.1 = ((bf16[32,64,512]{2,1,0:T(8,128)(2,1)}), bf16[32,64,512]{2,1,0:T(8,128)(2,1)S(1)}, u32[]{:S(2)}, u32[]{:S(2)}) async-start(bf16[32,64,512]{2,1,0:T(8,128)(2,1)} %bitcast.154), calls=%async_computation.1 | async-start | bytes 4194304 | tf_op jit(solution)/shard_map/all_to_all | solution.py:92
  37.0 621.0 %all-gather.3.cloned.1.call-start = ((), (), s32[]{:S(2)}) async-start(), calls=%async_computation.2 | async-start | bytes 10485760 | tf_op jit(solution)/shard_map/all_gather | solution.py:160
  37.3 0.6 copy-start.9
  84.5 6.4 copy-start.3
  87.3 3.7 copy-start.14
  87.3 3.7 copy-start.16
  91.0 2.6 copy-start.2
  118.9 0.8 copy-start.5
  189.6 0.8 copy-start.5
  260.2 0.8 copy-start.5
  330.9 0.8 copy-start.5
  376.2 4.9 copy-start.15
  381.2 4.3 copy-start.7
  381.2 4.3 copy-start.17
  385.4 7.9 %copy-start.6 = (bf16[2048,512]{0,1:T(8,128)(2,1)S(1)}, bf16[2048,512]{0,1:T(8,128)(2,1)}, u32[]{:S(2)}) copy-start(bf16[2048,512]{0,1:T(8,128)(2,1)} %copy.42) | copy-start | bytes 6291460
  385.4 7.9 %copy-start.12 = (f32[512]{0:T(512)S(1)}, f32[512]{0:T(512)}, u32[]{:S(2)}) copy-start(f32[512]{0:T(512)} %param.30) | copy-start | bytes 6148
  398.0 2.9 copy-start.8
  410.0 14.8 %collective-permute-start.1 = (bf16[2048,512]{1,0:T(8,128)(2,1)}, bf16[2048,512]{1,0:T(8,128)(2,1)S(1)}, u32[]{:S(2)}, u32[]{:S(2)}) collective-permute-start(bf16[2048,512]{1,0:T(8,128)(2,1)} %gather_fusion.3), channel_id=1, source_target_pairs={{0,4},{4,0},{8,12},{12,8},{16,20},{20,16},{24,28},{28,24},{1,5},{5... | collective-permute-start | bytes 6291464 | tf_op jit(solution)/shard_map/ppermute | solution.py:17
  423.5 1.2 collective-permute-start
  424.8 1.3 copy-start.13
  433.2 11.3 %copy-start.11 = (s32[2,1,2048]{2,1,0:T(1,128)S(1)}, s32[2,1,2048]{2,1,0:T(1,128)}, u32[]{:S(2)}) copy-start(s32[2,1,2048]{2,1,0:T(1,128)} %param.23) | copy-start | bytes 49156
  442.3 48.5 %collective-permute-start.3 = (bf16[2048,512]{1,0:T(8,128)(2,1)}, bf16[2048,512]{1,0:T(8,128)(2,1)}, u32[]{:S(2)}, u32[]{:S(2)}) collective-permute-start(bf16[2048,512]{1,0:T(8,128)(2,1)} %gather_fusion.5), channel_id=1, source_target_pairs={{0,8},{4,12},{8,0},{12,4},{16,24},{20,28},{24,16},{28,20},{1,9},{5... | collective-permute-start | bytes 6291464 | tf_op jit(solution)/shard_map/ppermute | solution.py:17
  456.3 34.5 %collective-permute-start.2 = (bf16[2048]{0:T(1024)(128)(2,1)S(1)}, bf16[2048]{0:T(1024)(128)(2,1)S(1)}, u32[]{:S(2)}, u32[]{:S(2)}) collective-permute-start(bf16[2048]{0:T(1024)(128)(2,1)S(1)} %convert_element_type.184), channel_id=1, source_target_pairs={{0,8},{4,12},{8,0},{12,4},{16,24},{20,28},{24,16},{28,20},{1,9},{5... | collective-permute-start | bytes 12296 | tf_op jit(solution)/shard_map/ppermute | solution.py:17
  708.7 4.1 copy-start.4
  708.7 11.8 %copy-start.1 = (bf16[1024,512]{1,0:T(8,128)(2,1)S(1)}, bf16[1024,512]{1,0:T(8,128)(2,1)}, u32[]{:S(2)}) copy-start(bf16[1024,512]{1,0:T(8,128)(2,1)} %param.17) | copy-start | bytes 3145732
Sparse Core Ops, SparseCore 0:
  509.7 148.3 all-gather.2
where the time goes:
time: 731 us; the launch traced here: 727 us
  local copies, waits for them, and re-layouts  331 us (45%)
  waiting for transfers between devices  181 us (25%)
  matrix products  120 us (16%)
  other arithmetic  49.8 us (7%)
  blocking collectives  15.1 us (2%)
  between operations  13.8 us (2%)
  starting transfers between devices  13.5 us (2%)
    gather x288, local copies, waits for them, and re-layouts  175 us
    all_gather x1, waiting for transfers between devices, body(): lax.all_gather(side_rows, 'grp', axis=0, tiled=True)  95.6 us
    dot_general x8, matrix products, block_sum(): jnp.dot(selector.astype(jnp.bfloat16), src_rows, preferred_element_type=j...  73.5 us
    all_to_all x1, waiting for transfers between devices, body(): lax.all_to_all(outgoing.reshape(owner_count, capacity, features), ('sub',...  45.9 us
    ppermute x4, waiting for transfers between devices, swapped(): lax.ppermute(shard, axis, [(i, i ^ 1 << apart) for i in range(lax.axis_si...  35.5 us
    scatter x3, local copies, waits for them, and re-layouts, invert(): jnp.zeros(perm.shape, jnp.int32).at[perm]  24.5 us
    dot_general x3, matrix products, refine(): lifted = jnp.dot(rounded, weight, preferred_element_type=jnp.float32)  19.3 us
    gather x2, local copies, waits for them, and re-layouts, body(): back_one[invert(perm_pair)].astype(jnp.float32)  15.2 us
  transfers between devices with their start and end apart: 7, of which 5 were waited for; matrix products, arithmetic and copies ran while one was open for 9% of the time, Pallas kernels for 0%

commit v1 on v0

v1 whole, which is shorter than its diff:
```python
import functools

import jax
import jax.numpy as jnp
from jax import lax
from jax.experimental import pallas as pl
from jax.experimental.pallas import tpu as pltpu
from jax.sharding import PartitionSpec as P

BLK = 128
TPB = 2
NBR = 8
LANES = 128
PAD = 16
EMPTY = 16384.0
LIMIT = 8192.0
AWAY = -8192.0
epsilon = 1e-05
f32 = jnp.float32
bf16 = jnp.bfloat16

VM = pl.BlockSpec(memory_space=pltpu.VMEM)
SM = pl.BlockSpec(memory_space=pltpu.SMEM)


def call(kernel, outs, args, specs=None, scratch=(), flops=0):
    return pl.pallas_call(
        kernel,
        out_shape=outs,
        in_specs=specs or [VM] * len(args),
        out_specs=jax.tree.map(lambda _: VM, outs),
        scratch_shapes=list(scratch),
        compiler_params=pltpu.CompilerParams(vmem_limit_bytes=44 << 20),
        cost_estimate=pl.CostEstimate(flops=flops, bytes_accessed=8 << 20, transcendentals=0),
    )(*args)


def rows_of(shape, start=0):
    return lax.broadcasted_iota(jnp.int32, shape, 0) + start


def lanes_of(shape, start=0):
    return lax.broadcasted_iota(jnp.int32, shape, 1) + start


def one_hot(mask):
    return jnp.where(mask, 1.0, 0.0).astype(bf16)


def spread(row):
    return jnp.broadcast_to(row, (LANES, LANES)).T


def dot(a, b):
    return jnp.dot(a, b, preferred_element_type=f32)


def half_silu(h):
    return h + h * jnp.tanh(h)


def picker(perm_ref, first, count, start, width):
    tiles = []
    for c in range(0, count, LANES):
        column = spread(perm_ref[:, pl.ds(pl.multiple_of(first + c, LANES), LANES)])
        wide = jnp.concatenate([column] * (width // LANES), axis=1)
        tiles.append(one_hot(wide == lanes_of((LANES, width), start)))
    return jnp.concatenate(tiles, axis=0)


def place_kernel(cap, owners_ref, nodes_ref, out_ref):
    owner_row = owners_ref[...]
    nodes = owner_row.shape[1]
    position = jnp.zeros((1, nodes), f32)
    for c in range(0, nodes, LANES):
        column = spread(owners_ref[:, c : c + LANES])
        wide = jnp.concatenate([column] * (nodes // LANES), axis=1)
        shape = (LANES, nodes)
        earlier = (wide == owner_row) & (rows_of(shape, c) < lanes_of(shape))
        position += jnp.sum(jnp.where(earlier, 1.0, 0.0), axis=0, keepdims=True)
    target = owner_row * cap + position.astype(jnp.int32)
    tile = 256

    @pl.loop(0, out_ref.shape[0] // tile)
    def _(t):
        start = pl.multiple_of(t * tile, tile)
        mask = rows_of((tile, nodes), start) == target
        weight = jnp.where(mask, 1.0, 0.0)
        filled = jnp.max(weight, axis=1, keepdims=True)
        rows = dot(weight.astype(bf16), nodes_ref[...])
        out_ref[pl.ds(start, tile), :] = jnp.where(filled > 0.5, rows, EMPTY).astype(bf16)


def compose_kernel(pair_ref, quad_ref, top_ref, two_ref, three_ref, parts, sums):
    width = pair_ref.shape[1]
    tile = 256

    def compose(outer, inner_row, out_ref):
        which = rows_of((8, width))
        high = (outer >> 7).astype(f32)
        low = (outer & 127).astype(f32)
        parts[...] = jnp.where(which == 0, high, jnp.where(which == 1, low, 0.0))
        sums[...] = jnp.zeros_like(sums)

        @pl.loop(0, width // tile)
        def _(t):
            start = pl.multiple_of(t * tile, tile)
            sel = one_hot(rows_of((tile, width), start) == inner_row)
            sums[...] += dot(parts[:, pl.ds(start, tile)].astype(bf16), sel)

        total = sums[...]
        out_ref[...] = (total[0:1] * 128.0 + total[1:2]).astype(jnp.int32)

    compose(pair_ref[...], quad_ref[...], two_ref)
    compose(two_ref[...], top_ref[...], three_ref)


def fine_kernel(
    tile_ref,
    arrived_ref,
    near_ref,
    pair_ref,
    edge_in_ref,
    edge_bias_ref,
    edge_out_ref,
    node_in_ref,
    node_bias_ref,
    node_out_ref,
    gain_ref,
    fine_ref,
    side_ref,
    slots,
    dst,
    src,
    agg,
    sels,
    near_rows,
):
    count, features = fine_ref.shape
    tile = 256

    @pl.loop(0, count // tile)
    def _(t):
        here = pl.ds(pl.multiple_of(t * tile, tile), tile)
        raw = arrived_ref[here, :].astype(f32)
        present = raw[:, 0:1] < LIMIT
        rows = jnp.where(present, raw, 0.0).astype(bf16)
        slots[here, :] = rows
        to_dst = (dot(rows, edge_in_ref[0]) + edge_bias_ref[...]) * 0.5
        dst[here, :] = to_dst.astype(bf16)
        from_src = dot(rows, edge_in_ref[1]) * 0.5
        src[here, :] = jnp.where(present, from_src, AWAY).astype(bf16)

    group = 16

    @pl.loop(0, count // BLK)
    def _(b):
        start = pl.multiple_of(b * BLK, BLK)
        near = near_ref[pl.ds(start, BLK), :]
        for j in range(TPB):
            for k in range(NBR):
                at = j * NBR + k
                mask = near[:, at : at + 1] == lanes_of((BLK, BLK))
                sels[k * BLK : (k + 1) * BLK, :] = one_hot(mask)
            first = pl.multiple_of(tile_ref[b, j] * BLK, BLK)
            near_rows[j * NBR * BLK : (j + 1) * NBR * BLK, :] = dot(
                sels[...], src[pl.ds(first, BLK), :]
            )
        for r in range(0, BLK, group):
            here = dst[pl.ds(start + r, group), :].astype(f32)
            total = jnp.zeros((group, features), f32)
            for at in range(TPB * NBR):
                total += half_silu(here + near_rows[at * BLK + r : at * BLK + r + group, :])
            agg[pl.ds(start + r, group), :] = total.astype(bf16)

    @pl.loop(0, count // tile)
    def _(t):
        here = pl.ds(pl.multiple_of(t * tile, tile), tile)
        rows = slots[here, :]
        message = dot(agg[here, :], edge_out_ref[...]).astype(bf16)
        lifted = dot(rows, node_in_ref[0]) + dot(message, node_in_ref[1]) + node_bias_ref[...]
        hidden = half_silu(lifted * 0.5).astype(bf16)
        delta = dot(hidden, node_out_ref[...])
        scale = lax.rsqrt(jnp.mean(delta * delta, axis=-1, keepdims=True) + epsilon)
        fine = rows.astype(f32) + gain_ref[...] * (delta * scale)
        present = arrived_ref[here, 0:LANES].astype(f32)[:, 0:1] < LIMIT
        fine_ref[here, :] = jnp.where(present, fine, EMPTY).astype(bf16)

    many = 512

    @pl.loop(0, count // many)
    def _(t):
        start = pl.multiple_of(t * many, many)
        sel = picker(pair_ref, start, many, 0, count)
        side_ref[pl.ds(start, many), :] = dot(sel, fine_ref[...]).astype(bf16)


def refined(total, count, weight):
    mean_rows = total * (1.0 / jnp.maximum(count, 1.0))
    lifted = dot(mean_rows.astype(bf16), weight)
    return mean_rows + half_silu(lifted * 0.5)


def widened(column, features):
    return jnp.concatenate([column] * (features // LANES), axis=1)


def put_counts(out_ref, rows, columns):
    features = out_ref.shape[1]
    per = features // LANES
    lines = []
    for c in range(0, len(columns), per):
        lines.append(jnp.concatenate([col.T[0:1, :] for col in columns[c : c + per]], axis=1))
    which = rows_of((PAD, features))
    tail = jnp.zeros((PAD, features), f32)
    for i, line in enumerate(lines):
        tail = jnp.where(which == i, line, tail)
    out_ref[rows : rows + PAD, :] = tail.astype(bf16)


def get_count(tail, c):
    features = tail.shape[1]
    line, lane = c // features, c % features
    return spread(tail[line : line + 1, lane : lane + LANES])


def one_kernel(pick_ref, side_ref, other_ref, weight_ref, level_ref, out_ref, wide):
    count, features = level_ref.shape
    tile = 256

    @pl.loop(0, count // tile)
    def _(t):
        here = pl.ds(pl.multiple_of(t * tile, tile), tile)
        a = side_ref[here, :].astype(f32)
        b = other_ref[here, :].astype(f32)
        in_a = a[:, 0:1] < LIMIT
        in_b = b[:, 0:1] < LIMIT
        total = jnp.where(in_a, a, 0.0) + jnp.where(in_b, b, 0.0)
        marks = jnp.where(in_a, 1.0, 0.0) + jnp.where(in_b, 1.0, 0.0)
        level = refined(total, marks, weight_ref[...]).astype(bf16)
        level_ref[here, :] = level
        wide[here, 0:features] = level
        wide[here, features : features + LANES] = jnp.broadcast_to(marks, (tile, LANES)).astype(
            bf16
        )

    picked = pick_ref.shape[1]
    many = 512
    columns = []
    for start in range(0, picked, many):
        sel = picker(pick_ref, start, many, 0, count)
        got = dot(sel, wide[...])
        out_ref[start : start + many, :] = got[:, 0:features].astype(bf16)
        for c in range(0, many, LANES):
            columns.append(got[c : c + LANES, features : features + LANES])
    put_counts(out_ref, picked, columns)


def two_kernel(mine_ref, other_ref, weight_ref, out_ref):
    count = out_ref.shape[0] - PAD
    features = out_ref.shape[1]
    mine_tail = mine_ref[count : count + PAD, :].astype(f32)
    other_tail = other_ref[count : count + PAD, :].astype(f32)
    columns = []
    for c in range(0, count, LANES):
        a, b = get_count(mine_tail, c), get_count(other_tail, c)
        columns.append(a + b)
        total = widened(a, features) * mine_ref[c : c + LANES, :].astype(f32) + widened(
            b, features
        ) * other_ref[c : c + LANES, :].astype(f32)
        level = refined(total, widened(a + b, features), weight_ref[...])
        out_ref[c : c + LANES, :] = level.astype(bf16)
    put_counts(out_ref, count, columns)


def pick_kernel(place_ref, pick_ref, mine_ref, other_ref, out_ref, wide):
    count = mine_ref.shape[0] - PAD
    features = out_ref.shape[1]
    picked = pick_ref.shape[1]
    core = place_ref[0] % 2
    for piece, (ref, half) in enumerate(((mine_ref, core), (other_ref, 1 - core))):
        base = pl.multiple_of(half * count, LANES)
        wide[pl.ds(base, count), 0:features] = ref[0:count, :]
        tail = ref[count : count + PAD, :].astype(f32)
        for c in range(0, count, LANES):
            wide[pl.ds(base + c, LANES), features : features + LANES] = get_count(tail, c).astype(
                bf16
            )
    sel = picker(pick_ref, 0, picked, 0, 2 * count)
    got = dot(sel, wide[...])
    out_ref[0:picked, :] = got[:, 0:features].astype(bf16)
    put_counts(
        out_ref,
        picked,
        [got[c : c + LANES, features : features + LANES] for c in range(0, picked, LANES)],
    )


def three_kernel(all_ref, weight_ref, out_ref):
    groups = all_ref.shape[0]
    count, features = out_ref.shape
    tails = [all_ref[g, count : count + PAD, :].astype(f32) for g in range(groups)]
    for c in range(0, count, LANES):
        total, marks = 0.0, 0.0
        for g in range(groups):
            got = get_count(tails[g], c)
            marks = marks + got
            total = total + widened(got, features) * all_ref[g, c : c + LANES, :].astype(f32)
        level = refined(total, widened(marks, features), weight_ref[...])
        out_ref[c : c + LANES, :] = level.astype(bf16)


def back_kernel(last, order, place_ref, perm_ref, base_ref, *refs):
    pieces, out_ref = refs[:-1], refs[-1]
    width = perm_ref.shape[1]
    size = width // len(pieces)
    tile = 256

    @pl.loop(0, out_ref.shape[0] // tile)
    def _(t):
        start = pl.multiple_of(t * tile, tile)
        here = pl.ds(start, tile)
        base = base_ref[here, :].astype(f32)
        total = base
        for piece, flip in zip(pieces, order):
            at = (place_ref[0] % len(pieces)) ^ flip
            targets = perm_ref[:, pl.ds(pl.multiple_of(at * size, LANES), size)]
            sel = one_hot(rows_of((tile, size), start) == targets)
            total = total + dot(sel, piece[0:size, :])
        absent = 0.0 if last else EMPTY
        out_ref[here, :] = jnp.where(base[:, 0:1] < LIMIT, total, absent).astype(bf16)


def swapped(shard, flip):
    count = lax.axis_size("sub")
    return lax.ppermute(shard, "sub", [(i, i ^ flip) for i in range(count)])


def body(
    node_rows,
    owners,
    tile_src,
    neighbors,
    pool_pair,
    pool_quad,
    pool_top,
    edge_in,
    edge_bias,
    edge_out,
    node_in,
    node_bias,
    node_out,
    out_gain,
    coarse,
):
    owner_count = lax.axis_size("sub") * lax.axis_size("grp")
    slot_rows = neighbors.shape[2]
    nodes, features = node_rows.shape
    cap = slot_rows // owner_count
    me = lax.axis_index("sub")
    half, quarter = slot_rows // 2, slot_rows // 4

    def shape(rows, dtype=bf16, width=features):
        return jax.ShapeDtypeStruct((rows, width), dtype)

    placed = call(
        functools.partial(place_kernel, cap),
        shape(slot_rows),
        (owners.reshape(1, nodes), node_rows),
        flops=2 * slot_rows * nodes * features,
    )
    arrived = lax.all_to_all(
        placed.reshape(owner_count, cap, features),
        ("sub", "grp"),
        split_axis=0,
        concat_axis=0,
        tiled=True,
    ).reshape(slot_rows, features)

    pair = pool_pair.reshape(1, slot_rows)
    quad = lax.dynamic_index_in_dim(pool_quad, me // 2, 0, keepdims=False)
    top = lax.dynamic_index_in_dim(pool_top, me // 4, 0, keepdims=False)
    place = me.reshape(1).astype(jnp.int32)
    quad_half = lax.dynamic_slice_in_dim(quad, (me % 2) * half, half, 1)
    top_quarter = lax.dynamic_slice_in_dim(top, (me % 4) * quarter, quarter, 1)
    to_two, to_three = call(
        compose_kernel,
        (shape(1, jnp.int32, slot_rows), shape(1, jnp.int32, slot_rows)),
        (pair, quad, top),
        scratch=[pltpu.VMEM((8, slot_rows), f32), pltpu.VMEM((8, slot_rows), f32)],
        flops=20 * 10**9,
    )

    fine, side = call(
        fine_kernel,
        (shape(slot_rows), shape(slot_rows)),
        (
            tile_src[0, 0],
            arrived,
            neighbors[0, 0],
            pair,
            edge_in,
            edge_bias.reshape(1, features),
            edge_out,
            node_in,
            node_bias.reshape(1, features),
            node_out,
            out_gain.reshape(1, features),
        ),
        specs=[SM] + [VM] * 10,
        scratch=[pltpu.VMEM((slot_rows, features), bf16)] * 4
        + [
            pltpu.VMEM((NBR * BLK, BLK), bf16),
            pltpu.VMEM((TPB * NBR * BLK, features), f32),
        ],
        flops=40 * 10**9,
    )
    other = swapped(side, 1)
    wide = pltpu.VMEM((slot_rows, features + LANES), bf16)
    level_one, mine = call(
        one_kernel,
        (shape(slot_rows), shape(half + PAD)),
        (quad_half, side, other, coarse[0]),
        scratch=[wide],
        flops=4 * 10**9,
    )
    other = swapped(mine, 2)
    back = functools.partial(back_kernel, False)
    wide_flops = 2 * slot_rows * slot_rows * features
    raised = call(
        functools.partial(back, (0,)),
        shape(slot_rows),
        (place, pair, fine, level_one),
        specs=[SM] + [VM] * 3,
        flops=wide_flops,
    )
    mine = call(two_kernel, shape(half + PAD), (mine, other, coarse[1]), flops=10**9)
    other = swapped(mine, 1)
    chosen = call(
        pick_kernel,
        shape(quarter + PAD),
        (place, top_quarter, mine, other),
        specs=[SM] + [VM] * 3,
        scratch=[wide],
        flops=10**9,
    )
    gathered = lax.all_gather(chosen, "grp", axis=0, tiled=False)
    raised = call(
        functools.partial(back, (0, 1)),
        shape(slot_rows),
        (place, to_two, raised, mine, other),
        specs=[SM] + [VM] * 4,
        flops=wide_flops,
    )
    mine = call(three_kernel, shape(quarter), (gathered, coarse[2]), flops=10**9)
    across = swapped(mine, 2)
    return call(
        functools.partial(back_kernel, True, (0, 2, 1, 3)),
        shape(slot_rows),
        (place, to_three, raised, mine, across, swapped(mine, 1), swapped(across, 1)),
        specs=[SM] + [VM] * 6,
        flops=wide_flops,
    )


def solution(mesh):
    in_specs = (
        P(("sub", "grp"), None),
        P(("sub", "grp")),
        P("sub", "grp", None, None),
        P("sub", "grp", None, None),
        P("sub", "grp", None),
        P(None, "grp", None),
        P(None, "grp", None),
        P(),
        P(),
        P(),
        P(),
        P(),
        P(),
        P(),
        P(),
    )
    out_specs = P(("sub", "grp"), None)
    return jax.shard_map(body, mesh=mesh, in_specs=in_specs, out_specs=out_specs, check_vma=False)
```

time: 731 us -> 247 us (0.34)
  local copies, waits for them, and re-layouts: 331 us -> 9.05 us
  matrix products: 120 us -> 0 us
  Pallas kernels: 0 us -> 82.1 us
  waiting for transfers between devices: 181 us -> 130 us
  other arithmetic: 49.8 us -> 0 us
  blocking collectives: 15.1 us -> 0 us
    gather x306 -> x0, local copies, waits for them, and re-layouts: 284 us -> none
    dot_general x17 -> x0, matrix products: 120 us -> none  [the longest x8 73.5 us: block_sum(): jnp.dot(selector.astype(jnp.bfloat16), src_rows, preferred_element_type=j...]
    pallas_call x0 -> x10, Pallas kernels: none -> 82.1 us  [call(): pl.pallas_call(kernel, out_shape=outs, in_specs=specs or [VM] * len(args)...]
    all_gather x1, waiting for transfers between devices: 95.6 us -> 45.6 us  [body(): gathered = lax.all_gather(chosen, 'grp', axis=0, tiled=False)]
    scatter x3 -> x0, local copies, waits for them, and re-layouts: 24.5 us -> none  [invert(): jnp.zeros(perm.shape, jnp.int32).at[perm]]
    convert_element_type x14 -> x0, other arithmetic: 17.3 us -> none  [the longest x1 4.63 us: body(): (present[:, None] * (slots.astype(jnp.float32) + out_gain * normed)).asty...]
    reduce_sum x12 -> x0, other arithmetic: 17.3 us -> none  [the longest x8 10.3 us: block_sum(): jnp.sum(jnp.where(selector, src_marks[None, :], 0.0), axis=1)]
    all_gather x1 -> x0, blocking collectives: 15.1 us -> none  [body(): lax.all_gather(side_counts.astype(jnp.bfloat16), 'grp', axis=0, tiled=True)]
  transfers between devices with their start and end apart: 7 -> 8, of which waited for: 5 -> 6; matrix products, arithmetic and copies ran while one was open for 9% -> 1% of each run, Pallas kernels for 0% -> 6%
where the time goes in v1:
time: 247 us
  waiting for transfers between devices  130 us (53%)
  Pallas kernels  82.1 us (33%)
  between operations  13.7 us (6%)
  starting transfers between devices  12.4 us (5%)
  local copies, waits for them, and re-layouts  9.05 us (4%)
    pallas_call x10, Pallas kernels, call(): pl.pallas_call(kernel, out_shape=outs, in_specs=specs or [VM] * len(args)...  82.1 us
    all_to_all x1, waiting for transfers between devices, body(): lax.all_to_all(placed.reshape(owner_count, cap, features), ('sub', 'grp')...  47 us
    all_gather x1, waiting for transfers between devices, body(): gathered = lax.all_gather(chosen, 'grp', axis=0, tiled=False)  45.6 us
    ppermute x6, waiting for transfers between devices, swapped(): return lax.ppermute(shard, 'sub', [(i, i ^ flip) for i in range(count)])  37.2 us
    all_to_all x1, starting transfers between devices, body(): lax.all_to_all(placed.reshape(owner_count, cap, features), ('sub', 'grp')...  7.43 us
    unnamed x39, local copies, waits for them, and re-layouts  7.33 us
  transfers between devices with their start and end apart: 8, of which 6 were waited for; matrix products, arithmetic and copies ran while one was open for 1% of the time, Pallas kernels for 6%

profile of v1, /device:TPU:0, one launch (start us, length us, event | category | flops | bytes accessed | tf_op | source)
XLA Modules:
  0.0 247.0 jit_solution(11249462283575076864)
XLA Ops:
  6.5 1.2 copy-done.2
  7.8 0.7 copy-done.8
  8.5 5.4 %shard_map.146 = bf16[2048,512]{1,0:T(8,128)(2,1)} custom-call(s32[1,1024]{1,0:T(1,128)S(1)} %bitcast.30, bf16[1024,512]{1,0:T(8,128)(2,1)S(1)} %copy-done.2), custom_call_target="tpu_custom_call" | custom-call | flops 2147483648 | bytes 8388608 | tf_op jit(solution)/shard_map/pallas_call | solution.py:27
  13.9 7.4 %all-to-all-start = ((bf16[32,64,512]{2,1,0:T(8,128)(2,1)}), bf16[32,64,512]{2,1,0:T(8,128)(2,1)}, u32[]{:S(2)}, u32[]{:S(2)}) async-start(bf16[32,64,512]{2,1,0:T(8,128)(2,1)} %bitcast.6), calls=%async_computation | async-start | bytes 4194304 | tf_op jit(solution)/shard_map/all_to_all | solution.py:372
  21.4 0.3 copy.16
  21.8 0.1 copy.17.tile_ref
  21.9 47.0 %all-to-all-done = bf16[32,64,512]{2,1,0:T(8,128)(2,1)} async-done(((bf16[32,64,512]{2,1,0:T(8,128)(2,1)}), bf16[32,64,512]{2,1,0:T(8,128)(2,1)}, u32[]{:S(2)}, u32[]{:S(2)}) %all-to-all-start) | async-done | bytes 2097184 | tf_op jit(solution)/shard_map/all_to_all | solution.py:372
  68.9 1.0 copy-done.5
  70.0 1.0 copy-done.6
  71.0 39.6 %shard_map.147 = (bf16[2048,512]{1,0:T(8,128)(2,1)S(1)}, bf16[2048,512]{1,0:T(8,128)(2,1)}) custom-call(s32[16,2]{1,0:T(8,128)S(1)} %copy.17.tile_ref, bf16[2048,512]{1,0:T(8,128)(2,1)} %bitcast.7.arrived_ref, s32[2048,16]{1,0:T(8,128)S(1)} %bitcast.25, s32[1,2048]{1,0:T(1,128)S(1)} %bitcast.27, bf16[2,512,512]{2,1,0:T(8,128)(2,1)S(1)} %copy-done.3, ...), custom_call_target="tpu_custom_call" | custom-call | flops 40000000000 | bytes 8388608 | tf_op jit(solution)/shard_map/pallas_call | solution.py:27
  110.6 1.3 copy-done.12
  112.0 1.0 collective-permute-start
  112.9 0.1 dynamic-slice_bitcast_fusion.2.pick_ref
  113.0 1.5 slice_bitcast_fusion
  114.5 2.6 %collective-permute-done.other_ref = bf16[2048,512]{1,0:T(8,128)(2,1)} collective-permute-done((bf16[2048,512]{1,0:T(8,128)(2,1)}, bf16[2048,512]{1,0:T(8,128)(2,1)}, u32[]{:S(2)}, u32[]{:S(2)}) %collective-permute-start) | collective-permute-done | bytes 2097184 | tf_op jit(solution)/shard_map/ppermute | solution.py:336
  117.1 9.6 %shard_map.148 = (bf16[2048,512]{1,0:T(8,128)(2,1)S(1)}, bf16[1040,512]{1,0:T(8,128)(2,1)S(1)}) custom-call(s32[1,1024]{1,0:T(1,128)S(1)} %dynamic-slice_bitcast_fusion.2.pick_ref, bf16[2048,512]{1,0:T(8,128)(2,1)} %get-tuple-element.14.side_ref, bf16[2048,512]{1,0:T(8,128)(2,1)} %collective-permute-done.other_ref, ...), custom_call_target="tpu_custom_call" | custom-call | flops 4000000000 | bytes 8388608 | tf_op jit(solution)/shard_map/pallas_call | solution.py:27
  126.6 2.2 collective-permute-start.1
  128.9 24.0 %collective-permute-done.1.other_ref = bf16[1040,512]{1,0:T(8,128)(2,1)S(1)} collective-permute-done((bf16[1040,512]{1,0:T(8,128)(2,1)S(1)}, bf16[1040,512]{1,0:T(8,128)(2,1)S(1)}, u32[]{:S(2)}, u32[]{:S(2)}) %collective-permute-start.1) | collective-permute-done | bytes 1064992 | tf_op jit(solution)/shard_map/ppermute | solution.py:336
  152.9 1.2 shard_map.150.refs_0_.mine_ref
  154.3 0.1 dynamic-slice_bitcast_fusion.3.pick_ref
  154.4 2.5 %collective-permute-done.2.refs_1_.other_ref = bf16[1040,512]{1,0:T(8,128)(2,1)S(1)} collective-permute-done((bf16[1040,512]{1,0:T(8,128)(2,1)S(1)}, bf16[1040,512]{1,0:T(8,128)(2,1)S(1)}, u32[]{:S(2)}, u32[]{:S(2)}) %collective-permute-start.2) | collective-permute-done | bytes 1064992 | tf_op jit(solution)/shard_map/ppermute | solution.py:336
  156.9 2.9 %shard_map.152 = bf16[528,512]{1,0:T(8,128)(2,1)} custom-call(s32[1]{0:T(128)} %bitcast.place_ref, s32[1,512]{1,0:T(1,128)S(1)} %dynamic-slice_bitcast_fusion.3.pick_ref, bf16[1040,512]{1,0:T(8,128)(2,1)S(1)} %shard_map.150.refs_0_.mine_ref, bf16[1040,512]{1,0:T(8,128)(2,1)S(1)} %collective-permute-done.2.refs_1_.other_ref), custom_call_target="tpu_custom_call" | custom-call | flops 1000000000 | bytes 8388608 | tf_op jit(solution)/shard_map/pallas_call | solution.py:27
  159.9 45.6 %all-gather.3.cloned.1.call-done = bf16[2112,512]{1,0:T(8,128)(2,1)} async-done(((bf16[528,512]{1,0:T(8,128)(2,1)}), bf16[2112,512]{1,0:T(8,128)(2,1)}) %all-gather.3.cloned.1.call-update) | async-done | bytes 2162704 | tf_op jit(solution)/shard_map/all_gather | solution.py:447
  205.6 1.6 copy-done.1
  207.2 0.9 shard_map.153.refs_0_
  208.1 1.5 collective-permute-start.3
  209.6 4.1 %shard_map.145 = (s32[1,2048]{1,0:T(1,128)S(1)}, s32[1,2048]{1,0:T(1,128)S(1)}) custom-call(s32[1,2048]{1,0:T(1,128)S(1)} %bitcast.28, s32[1,2048]{1,0:T(1,128)S(1)} %dynamic-slice_bitcast_fusion.1.quad_ref, s32[1,2048]{1,0:T(1,128)S(1)} %dynamic-slice_bitcast_fusion.top_ref), custom_call_target="tpu_custom_call" | custom-call | flops 20000000000 | bytes 8388608 | tf_op jit(solution)/shard_map/pallas_call | solution.py:27
  213.7 0.1 collective-permute-start.4
  213.8 8.0 %collective-permute-done.3.refs_1_ = bf16[512,512]{1,0:T(8,128)(2,1)S(1)} collective-permute-done((bf16[512,512]{1,0:T(8,128)(2,1)S(1)}, bf16[512,512]{1,0:T(8,128)(2,1)S(1)}, u32[]{:S(2)}, u32[]{:S(2)}) %collective-permute-start.3) | collective-permute-done | bytes 524320 | tf_op jit(solution)/shard_map/ppermute | solution.py:336
  221.8 5.7 %shard_map.149.base_ref = bf16[2048,512]{1,0:T(8,128)(2,1)S(1)} custom-call(s32[1]{0:T(128)} %bitcast.place_ref, s32[1,2048]{1,0:T(1,128)S(1)} %bitcast.29, bf16[2048,512]{1,0:T(8,128)(2,1)S(1)} %copy-done.13, bf16[2048,512]{1,0:T(8,128)(2,1)S(1)} %copy-done.15), custom_call_target="tpu_custom_call" | custom-call | flops 4294967296 | bytes 8388608 | tf_op jit(solution)/shard_map/pallas_call | solution.py:27
  227.5 5.7 %shard_map.151.base_ref = bf16[2048,512]{1,0:T(8,128)(2,1)S(1)} custom-call(s32[1]{0:T(128)} %bitcast.place_ref, s32[1,2048]{1,0:T(1,128)S(1)} %get-tuple-element.12.perm_ref, bf16[2048,512]{1,0:T(8,128)(2,1)S(1)} %shard_map.149.base_ref, bf16[1040,512]{1,0:T(8,128)(2,1)S(1)} %shard_map.150.refs_0_.mine_ref, ...), custom_call_target="tpu_custom_call" | custom-call | flops 4294967296 | bytes 8388608 | tf_op jit(solution)/shard_map/pallas_call | solution.py:27
  233.2 7.0 %shard_map.154 = bf16[2048,512]{1,0:T(8,128)(2,1)} custom-call(s32[1]{0:T(128)} %bitcast.place_ref, s32[1,2048]{1,0:T(1,128)S(1)} %get-tuple-element.11.perm_ref, bf16[2048,512]{1,0:T(8,128)(2,1)S(1)} %shard_map.151.base_ref, bf16[512,512]{1,0:T(8,128)(2,1)S(1)} %shard_map.153.refs_0_, bf16[512,512]{1,0:T(8,128)(2,1)S(1)} %collective-permute-done.3.refs_1_, ...), custom_call_target="tpu_custom_call" | custom-call | flops 4294967296 | bytes 8388608 | tf_op jit(solution)/shard_map/pallas_call | solution.py:27
  (40 shorter events, 0.2 us)
Async XLA Ops:
  6.5 106.4 %copy-start = (s32[4,1,2048]{2,1,0:T(1,128)S(1)}, s32[4,1,2048]{2,1,0:T(1,128)}, u32[]{:S(2)}) copy-start(s32[4,1,2048]{2,1,0:T(1,128)} %param.20) | copy-start | bytes 98308
  6.5 1.2 copy-start.2
  7.8 0.7 copy-start.8
  13.9 7.6 %copy-start.16 = (s32[1,1,2048,16]{2,3,1,0:T(8,128)S(1)}, s32[1,1,2048,16]{2,3,1,0:T(8,128)}, u32[]{:S(2)}) copy-start(s32[1,1,2048,16]{2,3,1,0:T(8,128)} %param.18) | copy-start | bytes 393220
  13.9 7.9 %copy-start.18 = (s32[1,1,16,2]{2,3,1,0:T(2,128)S(1)}, s32[1,1,16,2]{2,3,1,0:T(2,128)}, u32[]{:S(2)}) copy-start(s32[1,1,16,2]{2,3,1,0:T(2,128)} %param.17) | copy-start | bytes 388
  13.9 55.0 %copy-start.3 = (bf16[2,512,512]{2,1,0:T(8,128)(2,1)S(1)}, bf16[2,512,512]{2,1,0:T(8,128)(2,1)}, u32[]{:S(2)}) copy-start(bf16[2,512,512]{2,1,0:T(8,128)(2,1)} %edge_in_ref.1) | copy-start | bytes 3145732
  13.9 55.0 %copy-start.4 = (bf16[2,512,512]{2,1,0:T(8,128)(2,1)S(1)}, bf16[2,512,512]{2,1,0:T(8,128)(2,1)}, u32[]{:S(2)}) copy-start(bf16[2,512,512]{2,1,0:T(8,128)(2,1)} %node_in_ref.1) | copy-start | bytes 3145732
  13.9 55.0 %copy-start.7 = (s32[1,1,2048]{2,1,0:T(1,128)S(1)}, s32[1,1,2048]{2,1,0:T(1,128)}, u32[]{:S(2)}) copy-start(s32[1,1,2048]{2,1,0:T(1,128)} %param.19) | copy-start | bytes 24580
  13.9 55.0 %copy-start.9 = (f32[512]{0:T(512)S(1)}, f32[512]{0:T(512)}, u32[]{:S(2)}) copy-start(f32[512]{0:T(512)} %param.23) | copy-start | bytes 6148
  13.9 55.0 %copy-start.10 = (f32[512]{0:T(512)S(1)}, f32[512]{0:T(512)}, u32[]{:S(2)}) copy-start(f32[512]{0:T(512)} %param.26) | copy-start | bytes 6148
  13.9 55.0 %copy-start.11 = (f32[512]{0:T(512)S(1)}, f32[512]{0:T(512)}, u32[]{:S(2)}) copy-start(f32[512]{0:T(512)} %param.28) | copy-start | bytes 6148
  13.9 54.9 %all-to-all-start = ((bf16[32,64,512]{2,1,0:T(8,128)(2,1)}), bf16[32,64,512]{2,1,0:T(8,128)(2,1)}, u32[]{:S(2)}, u32[]{:S(2)}) async-start(bf16[32,64,512]{2,1,0:T(8,128)(2,1)} %bitcast.6), calls=%async_computation | async-start | bytes 4194304 | tf_op jit(solution)/shard_map/all_to_all | solution.py:372
  21.4 184.2 %all-gather.3.cloned.1.call-start = ((), (), s32[]{:S(2)}) async-start(), calls=%async_computation.1 | async-start | bytes 2703360 | tf_op jit(solution)/shard_map/all_gather | solution.py:447
  68.9 1.0 copy-start.5
  70.0 1.0 copy-start.6
  110.6 1.3 copy-start.12
  112.0 5.1 %collective-permute-start = (bf16[2048,512]{1,0:T(8,128)(2,1)}, bf16[2048,512]{1,0:T(8,128)(2,1)}, u32[]{:S(2)}, u32[]{:S(2)}) collective-permute-start(bf16[2048,512]{1,0:T(8,128)(2,1)} %get-tuple-element.14.side_ref), channel_id=1, source_target_pairs={{0,4},{4,0},{8,12},{12,8},{16,20},{20,16},{24,28},{28,24},{1,5},{5... | collective-permute-start | bytes 6291464 | tf_op jit(solution)/shard_map/ppermute | solution.py:336
  126.6 27.5 %copy-start.14 = (bf16[2048,512]{1,0:T(8,128)(2,1)}, bf16[2048,512]{1,0:T(8,128)(2,1)S(1)}, u32[]{:S(2)}) copy-start(bf16[2048,512]{1,0:T(8,128)(2,1)S(1)} %get-tuple-element.15.refs_0_) | copy-start | bytes 6291460
  126.6 27.7 %copy-start.17 = (s32[2,1,2048]{2,1,0:T(1,128)S(1)}, s32[2,1,2048]{2,1,0:T(1,128)}, u32[]{:S(2)}) copy-start(s32[2,1,2048]{2,1,0:T(1,128)} %param.21) | copy-start | bytes 49156
  126.6 26.3 %collective-permute-start.1 = (bf16[1040,512]{1,0:T(8,128)(2,1)S(1)}, bf16[1040,512]{1,0:T(8,128)(2,1)S(1)}, u32[]{:S(2)}, u32[]{:S(2)}) collective-permute-start(bf16[1040,512]{1,0:T(8,128)(2,1)S(1)} %get-tuple-element.16.mine_ref), channel_id=1, source_target_pairs={{0,8},{4,12},{8,0},{12,4},{16,24},{20,28},{24,16},{28,20},{1,9},{5... | collective-permute-start | bytes 3194888 | tf_op jit(solution)/shard_map/ppermute | solution.py:336
  154.2 2.7 %collective-permute-start.2 = (bf16[1040,512]{1,0:T(8,128)(2,1)S(1)}, bf16[1040,512]{1,0:T(8,128)(2,1)S(1)}, u32[]{:S(2)}, u32[]{:S(2)}) collective-permute-start(bf16[1040,512]{1,0:T(8,128)(2,1)S(1)} %shard_map.150.refs_0_.mine_ref), channel_id=1, source_target_pairs={{0,4},{4,0},{8,12},{12,8},{16,20},{20,16},{24,28},{28,24},{1,5},{5... | collective-permute-start | bytes 3194888 | tf_op jit(solution)/shard_map/ppermute | solution.py:336
  205.6 1.6 copy-start.1
  208.1 13.8 %copy-start.13 = (bf16[2048,512]{1,0:T(8,128)(2,1)S(1)}, bf16[2048,512]{1,0:T(8,128)(2,1)}, u32[]{:S(2)}) copy-start(bf16[2048,512]{1,0:T(8,128)(2,1)} %copy-done.12) | copy-start | bytes 6291460
  208.1 13.8 %copy-start.15 = (bf16[2048,512]{1,0:T(8,128)(2,1)S(1)}, bf16[2048,512]{1,0:T(8,128)(2,1)}, u32[]{:S(2)}) copy-start(bf16[2048,512]{1,0:T(8,128)(2,1)} %copy-done.14) | copy-start | bytes 6291460
  208.1 13.7 %collective-permute-start.3 = (bf16[512,512]{1,0:T(8,128)(2,1)S(1)}, bf16[512,512]{1,0:T(8,128)(2,1)S(1)}, u32[]{:S(2)}, u32[]{:S(2)}) collective-permute-start(bf16[512,512]{1,0:T(8,128)(2,1)S(1)} %shard_map.153.refs_0_), channel_id=1, source_target_pairs={{0,8},{4,12},{8,0},{12,4},{16,24},{20,28},{24,16},{28,20},{1,9},{5... | collective-permute-start | bytes 1572872 | tf_op jit(solution)/shard_map/ppermute | solution.py:336
  213.7 19.4 %collective-permute-start.4 = (bf16[512,512]{1,0:T(8,128)(2,1)S(1)}, bf16[512,512]{1,0:T(8,128)(2,1)S(1)}, u32[]{:S(2)}, u32[]{:S(2)}) collective-permute-start(bf16[512,512]{1,0:T(8,128)(2,1)S(1)} %shard_map.153.refs_0_), channel_id=1, source_target_pairs={{0,4},{4,0},{8,12},{12,8},{16,20},{20,16},{24,28},{28,24},{1,5},{5... | collective-permute-start | bytes 1572872 | tf_op jit(solution)/shard_map/ppermute | solution.py:336
  221.8 11.4 %collective-permute-start.5 = (bf16[512,512]{1,0:T(8,128)(2,1)S(1)}, bf16[512,512]{1,0:T(8,128)(2,1)S(1)}, u32[]{:S(2)}, u32[]{:S(2)}) collective-permute-start(bf16[512,512]{1,0:T(8,128)(2,1)S(1)} %collective-permute-done.3.refs_1_), channel_id=1, source_target_pairs={{0,4},{4,0},{8,12},{12,8},{16,20},{20,16},{24,28},{28,24},{1,5},{5... | collective-permute-start | bytes 1572872 | tf_op jit(solution)/shard_map/ppermute | solution.py:336
Sparse Core Ops, SparseCore 0:
  160.0 45.5 all-gather.2

commit v2 on v1

--- a/solution.py
+++ b/solution.py
@@ -165,12 +165,13 @@
             first = pl.multiple_of(tile_ref[b, j] * BLK, BLK)
             near_rows[j * NBR * BLK : (j + 1) * NBR * BLK, :] = dot(
                 sels[...], src[pl.ds(first, BLK), :]
-            )
+            ).astype(bf16)
         for r in range(0, BLK, group):
-            here = dst[pl.ds(start + r, group), :].astype(f32)
+            here = dst[pl.ds(start + r, group), :]
             total = jnp.zeros((group, features), f32)
             for at in range(TPB * NBR):
-                total += half_silu(here + near_rows[at * BLK + r : at * BLK + r + group, :])
+                term = half_silu(here + near_rows[at * BLK + r : at * BLK + r + group, :])
+                total += term.astype(f32)
             agg[pl.ds(start + r, group), :] = total.astype(bf16)
 
     @pl.loop(0, count // tile)
@@ -390,6 +391,7 @@
         scratch=[pltpu.VMEM((8, slot_rows), f32), pltpu.VMEM((8, slot_rows), f32)],
         flops=20 * 10**9,
     )
+    arrived, to_two, to_three = lax.optimization_barrier((arrived, to_two, to_three))
 
     fine, side = call(
         fine_kernel,
@@ -411,7 +413,7 @@
         scratch=[pltpu.VMEM((slot_rows, features), bf16)] * 4
         + [
             pltpu.VMEM((NBR * BLK, BLK), bf16),
-            pltpu.VMEM((TPB * NBR * BLK, features), f32),
+            pltpu.VMEM((TPB * NBR * BLK, features), bf16),
         ],
         flops=40 * 10**9,
     )
@@ -434,6 +436,7 @@
         specs=[SM] + [VM] * 3,
         flops=wide_flops,
     )
+    other, raised = lax.optimization_barrier((other, raised))
     mine = call(two_kernel, shape(half + PAD), (mine, other, coarse[1]), flops=10**9)
     other = swapped(mine, 1)
     chosen = call(
@@ -452,6 +455,7 @@
         specs=[SM] + [VM] * 4,
         flops=wide_flops,
     )
+    gathered, raised = lax.optimization_barrier((gathered, raised))
     mine = call(three_kernel, shape(quarter), (gathered, coarse[2]), flops=10**9)
     across = swapped(mine, 2)
     return call(

time: 247 us -> 237 us (0.960)
  waiting for transfers between devices: 130 us -> 116 us
  local copies, waits for them, and re-layouts: 9.05 us -> 13.3 us
    all_gather x1, waiting for transfers between devices: 45.6 us -> 37.1 us  [body(): gathered = lax.all_gather(chosen, 'grp', axis=0, tiled=False)]
    all_to_all x1, waiting for transfers between devices: 47 us -> 42.1 us  [body(): lax.all_to_all(placed.reshape(owner_count, cap, features), ('sub', 'grp')...]
    unnamed x39 -> x41, local copies, waits for them, and re-layouts: 7.33 us -> 10.2 us
  transfers between devices with their start and end apart: 8 -> 8, of which waited for: 6 -> 7; matrix products, arithmetic and copies ran while one was open for 1% -> 1% of each run, Pallas kernels for 6% -> 7%
where the time goes in v2:
time: 237 us; the launch traced here: 236 us
  waiting for transfers between devices  116 us (49%)
  Pallas kernels  80.6 us (34%)
  between operations  13.6 us (6%)
  local copies, waits for them, and re-layouts  13.3 us (6%)
  starting transfers between devices  12.3 us (5%)
    pallas_call x10, Pallas kernels, call(): pl.pallas_call(kernel, out_shape=outs, in_specs=specs or [VM] * len(args)...  80.6 us
    all_to_all x1, waiting for transfers between devices, body(): lax.all_to_all(placed.reshape(owner_count, cap, features), ('sub', 'grp')...  42.1 us
    all_gather x1, waiting for transfers between devices, body(): gathered = lax.all_gather(chosen, 'grp', axis=0, tiled=False)  37.1 us
    ppermute x6, waiting for transfers between devices, swapped(): return lax.ppermute(shard, 'sub', [(i, i ^ flip) for i in range(count)])  36.9 us
    unnamed x41, local copies, waits for them, and re-layouts  10.2 us
    all_to_all x1, starting transfers between devices, body(): lax.all_to_all(placed.reshape(owner_count, cap, features), ('sub', 'grp')...  7.43 us
    ppermute x6, starting transfers between devices, swapped(): return lax.ppermute(shard, 'sub', [(i, i ^ flip) for i in range(count)])  4.81 us
  transfers between devices with their start and end apart: 8, of which 7 were waited for; matrix products, arithmetic and copies ran while one was open for 1% of the time, Pallas kernels for 7%

profile of v2, /device:TPU:0, one launch (start us, length us, event | category | flops | bytes accessed | tf_op | source)
XLA Modules:
  0.0 236.0 jit_solution(17371292247774871786)
XLA Ops:
  6.5 1.2 copy-done.1
  7.8 0.7 copy-done.7
  8.4 5.4 %shard_map.145 = bf16[2048,512]{1,0:T(8,128)(2,1)} custom-call(s32[1,1024]{1,0:T(1,128)S(1)} %bitcast.30, bf16[1024,512]{1,0:T(8,128)(2,1)S(1)} %copy-done.1), custom_call_target="tpu_custom_call" | custom-call | flops 2147483648 | bytes 8388608 | tf_op jit(solution)/shard_map/pallas_call | solution.py:27
  13.9 7.4 %all-to-all-start = ((bf16[32,64,512]{2,1,0:T(8,128)(2,1)}), bf16[32,64,512]{2,1,0:T(8,128)(2,1)}, u32[]{:S(2)}, u32[]{:S(2)}) async-start(bf16[32,64,512]{2,1,0:T(8,128)(2,1)} %bitcast.2), calls=%async_computation | async-start | bytes 4194304 | tf_op jit(solution)/shard_map/all_to_all | solution.py:373
  21.8 0.7 dynamic-slice_bitcast_fusion
  22.6 4.1 %shard_map.146 = (s32[1,2048]{1,0:T(1,128)S(1)}, s32[1,2048]{1,0:T(1,128)S(1)}) custom-call(s32[1,2048]{1,0:T(1,128)S(1)} %bitcast.27, s32[1,2048]{1,0:T(1,128)S(1)} %get-tuple-element.35.quad_ref, s32[1,2048]{1,0:T(1,128)S(1)} %get-tuple-element.34.top_ref), custom_call_target="tpu_custom_call" | custom-call | flops 20000000000 | bytes 8388608 | tf_op jit(solution)/shard_map/pallas_call | solution.py:27
  26.7 42.1 %all-to-all-done = bf16[32,64,512]{2,1,0:T(8,128)(2,1)} async-done(((bf16[32,64,512]{2,1,0:T(8,128)(2,1)}), bf16[32,64,512]{2,1,0:T(8,128)(2,1)}, u32[]{:S(2)}, u32[]{:S(2)}) %all-to-all-start) | async-done | bytes 2097184 | tf_op jit(solution)/shard_map/all_to_all | solution.py:373
  68.9 1.0 copy-done.4
  69.9 1.0 copy-done.5
  70.9 38.1 %shard_map.147 = (bf16[2048,512]{1,0:T(8,128)(2,1)S(1)}, bf16[2048,512]{1,0:T(8,128)(2,1)}) custom-call(s32[16,2]{1,0:T(8,128)S(1)} %copy.17.tile_ref, bf16[2048,512]{1,0:T(8,128)(2,1)} %bitcast.3.arrived_ref, s32[2048,16]{1,0:T(8,128)S(1)} %bitcast.25, s32[1,2048]{1,0:T(1,128)S(1)} %bitcast.28, bf16[2,512,512]{2,1,0:T(8,128)(2,1)S(1)} %copy-done.2, ...), custom_call_target="tpu_custom_call" | custom-call | flops 40000000000 | bytes 8388608 | tf_op jit(solution)/shard_map/pallas_call | solution.py:27
  109.0 1.3 copy-done.15
  110.3 1.0 collective-permute-start
  111.3 0.8 dynamic-slice_bitcast_fusion.2.pick_ref
  112.1 1.5 slice_bitcast_fusion
  113.6 1.9 collective-permute-done.other_ref
  115.5 9.7 %shard_map.148 = (bf16[2048,512]{1,0:T(8,128)(2,1)S(1)}, bf16[1040,512]{1,0:T(8,128)(2,1)S(1)}) custom-call(s32[1,1024]{1,0:T(1,128)S(1)} %dynamic-slice_bitcast_fusion.2.pick_ref, bf16[2048,512]{1,0:T(8,128)(2,1)} %get-tuple-element.22.side_ref, bf16[2048,512]{1,0:T(8,128)(2,1)} %collective-permute-done.other_ref, ...), custom_call_target="tpu_custom_call" | custom-call | flops 4000000000 | bytes 8388608 | tf_op jit(solution)/shard_map/pallas_call | solution.py:27
  125.2 2.2 collective-permute-start.1
  127.4 5.7 %shard_map.149.base_ref = bf16[2048,512]{1,0:T(8,128)(2,1)S(1)} custom-call(s32[1]{0:T(128)} %bitcast.place_ref, s32[1,2048]{1,0:T(1,128)S(1)} %bitcast.29, bf16[2048,512]{1,0:T(8,128)(2,1)S(1)} %copy-done.16, bf16[2048,512]{1,0:T(8,128)(2,1)S(1)} %get-tuple-element.25.refs_0_), custom_call_target="tpu_custom_call" | custom-call | flops 4294967296 | bytes 8388608 | tf_op jit(solution)/shard_map/pallas_call | solution.py:27
  133.1 18.3 %collective-permute-done.1.other_ref = bf16[1040,512]{1,0:T(8,128)(2,1)S(1)} collective-permute-done((bf16[1040,512]{1,0:T(8,128)(2,1)S(1)}, bf16[1040,512]{1,0:T(8,128)(2,1)S(1)}, u32[]{:S(2)}, u32[]{:S(2)}) %collective-permute-start.1) | collective-permute-done | bytes 1064992 | tf_op jit(solution)/shard_map/ppermute | solution.py:337
  151.4 1.2 shard_map.150.mine_ref.refs_0_
  152.8 2.6 %collective-permute-done.2.other_ref.refs_1_ = bf16[1040,512]{1,0:T(8,128)(2,1)S(1)} collective-permute-done((bf16[1040,512]{1,0:T(8,128)(2,1)S(1)}, bf16[1040,512]{1,0:T(8,128)(2,1)S(1)}, u32[]{:S(2)}, u32[]{:S(2)}) %collective-permute-start.2) | collective-permute-done | bytes 1064992 | tf_op jit(solution)/shard_map/ppermute | solution.py:337
  155.4 2.9 %shard_map.151 = bf16[528,512]{1,0:T(8,128)(2,1)} custom-call(s32[1]{0:T(128)} %bitcast.place_ref, s32[1,512]{1,0:T(1,128)S(1)} %dynamic-slice_bitcast_fusion.3.pick_ref, bf16[1040,512]{1,0:T(8,128)(2,1)S(1)} %shard_map.150.mine_ref.refs_0_, bf16[1040,512]{1,0:T(8,128)(2,1)S(1)} %collective-permute-done.2.other_ref.refs_1_), custom_call_target="tpu_custom_call" | custom-call | flops 1000000000 | bytes 8388608 | tf_op jit(solution)/shard_map/pallas_call | solution.py:27
  158.4 1.6 copy-done.12
  159.9 5.7 %shard_map.152.base_ref = bf16[2048,512]{1,0:T(8,128)(2,1)S(1)} custom-call(s32[1]{0:T(128)} %bitcast.place_ref, s32[1,2048]{1,0:T(1,128)S(1)} %get-tuple-element.27.perm_ref, bf16[2048,512]{1,0:T(8,128)(2,1)S(1)} %copy-done.12, bf16[1040,512]{1,0:T(8,128)(2,1)S(1)} %shard_map.150.mine_ref.refs_0_, bf16[1040,512]{1,0:T(8,128)(2,1)S(1)} %collective-permute-done.2.other_ref.refs_1_), custom_call_target="tpu_custom_call" | custom-call | flops 4294967296 | bytes 8388608 | tf_op jit(solution)/shard_map/pallas_call | solution.py:27
  165.6 1.3 copy-done.13
  166.9 37.1 %all-gather.3.cloned.1.call-done = bf16[2112,512]{1,0:T(8,128)(2,1)} async-done(((bf16[528,512]{1,0:T(8,128)(2,1)}), bf16[2112,512]{1,0:T(8,128)(2,1)}) %all-gather.3.cloned.1.call-update) | async-done | bytes 2162704 | tf_op jit(solution)/shard_map/all_gather | solution.py:450
  204.0 1.6 copy-done
  205.6 0.9 shard_map.153.refs_0_
  206.5 1.5 collective-permute-start.3
  208.0 12.2 %collective-permute-done.3.refs_1_ = bf16[512,512]{1,0:T(8,128)(2,1)S(1)} collective-permute-done((bf16[512,512]{1,0:T(8,128)(2,1)S(1)}, bf16[512,512]{1,0:T(8,128)(2,1)S(1)}, u32[]{:S(2)}, u32[]{:S(2)}) %collective-permute-start.3) | collective-permute-done | bytes 524320 | tf_op jit(solution)/shard_map/ppermute | solution.py:337
  220.2 1.9 collective-permute-done.5.refs_3_
  222.2 7.0 %shard_map.154 = bf16[2048,512]{1,0:T(8,128)(2,1)} custom-call(s32[1]{0:T(128)} %bitcast.place_ref, s32[1,2048]{1,0:T(1,128)S(1)} %get-tuple-element.20.perm_ref, bf16[2048,512]{1,0:T(8,128)(2,1)S(1)} %copy-done.14, bf16[512,512]{1,0:T(8,128)(2,1)S(1)} %shard_map.153.refs_0_, bf16[512,512]{1,0:T(8,128)(2,1)S(1)} %collective-permute-done.3.refs_1_, ...), custom_call_target="tpu_custom_call" | custom-call | flops 4294967296 | bytes 8388608 | tf_op jit(solution)/shard_map/pallas_call | solution.py:27
  (41 shorter events, 0.7 us)
Async XLA Ops:
  6.5 1.2 copy-start.1
  7.8 0.7 copy-start.7
  13.9 7.5 %copy-start.17 = (s32[1,1,2048,16]{2,3,1,0:T(8,128)S(1)}, s32[1,1,2048,16]{2,3,1,0:T(8,128)}, u32[]{:S(2)}) copy-start(s32[1,1,2048,16]{2,3,1,0:T(8,128)} %param.18) | copy-start | bytes 393220
  13.9 7.9 %copy-start.19 = (s32[1,1,16,2]{2,3,1,0:T(2,128)S(1)}, s32[1,1,16,2]{2,3,1,0:T(2,128)}, u32[]{:S(2)}) copy-start(s32[1,1,16,2]{2,3,1,0:T(2,128)} %param.17) | copy-start | bytes 388
  13.9 8.0 %copy-start.18 = (s32[2,1,2048]{2,1,0:T(1,128)S(1)}, s32[2,1,2048]{2,1,0:T(1,128)}, u32[]{:S(2)}) copy-start(s32[2,1,2048]{2,1,0:T(1,128)} %param.21) | copy-start | bytes 49156
  13.9 8.7 %copy-start.6 = (s32[1,1,2048]{2,1,0:T(1,128)S(1)}, s32[1,1,2048]{2,1,0:T(1,128)}, u32[]{:S(2)}) copy-start(s32[1,1,2048]{2,1,0:T(1,128)} %param.19) | copy-start | bytes 24580
  13.9 54.9 %all-to-all-start = ((bf16[32,64,512]{2,1,0:T(8,128)(2,1)}), bf16[32,64,512]{2,1,0:T(8,128)(2,1)}, u32[]{:S(2)}, u32[]{:S(2)}) async-start(bf16[32,64,512]{2,1,0:T(8,128)(2,1)} %bitcast.2), calls=%async_computation | async-start | bytes 4194304 | tf_op jit(solution)/shard_map/all_to_all | solution.py:373
  21.3 182.7 %all-gather.3.cloned.1.call-start = ((), (), s32[]{:S(2)}) async-start(), calls=%async_computation.1 | async-start | bytes 2703360 | tf_op jit(solution)/shard_map/all_gather | solution.py:450
  22.5 46.3 %copy-start.2 = (bf16[2,512,512]{2,1,0:T(8,128)(2,1)S(1)}, bf16[2,512,512]{2,1,0:T(8,128)(2,1)}, u32[]{:S(2)}) copy-start(bf16[2,512,512]{2,1,0:T(8,128)(2,1)} %edge_in_ref.1) | copy-start | bytes 3145732
  22.5 46.3 %copy-start.3 = (bf16[2,512,512]{2,1,0:T(8,128)(2,1)S(1)}, bf16[2,512,512]{2,1,0:T(8,128)(2,1)}, u32[]{:S(2)}) copy-start(bf16[2,512,512]{2,1,0:T(8,128)(2,1)} %node_in_ref.1) | copy-start | bytes 3145732
  22.6 46.3 %copy-start.8 = (f32[512]{0:T(512)S(1)}, f32[512]{0:T(512)}, u32[]{:S(2)}) copy-start(f32[512]{0:T(512)} %param.23) | copy-start | bytes 6148
  22.6 46.3 %copy-start.9 = (f32[512]{0:T(512)S(1)}, f32[512]{0:T(512)}, u32[]{:S(2)}) copy-start(f32[512]{0:T(512)} %param.26) | copy-start | bytes 6148
  22.6 46.3 %copy-start.10 = (f32[512]{0:T(512)S(1)}, f32[512]{0:T(512)}, u32[]{:S(2)}) copy-start(f32[512]{0:T(512)} %param.28) | copy-start | bytes 6148
  68.8 1.0 copy-start.4
  69.9 1.0 copy-start.5
  109.0 1.3 copy-start.15
  110.3 5.1 %collective-permute-start = (bf16[2048,512]{1,0:T(8,128)(2,1)}, bf16[2048,512]{1,0:T(8,128)(2,1)}, u32[]{:S(2)}, u32[]{:S(2)}) collective-permute-start(bf16[2048,512]{1,0:T(8,128)(2,1)} %get-tuple-element.22.side_ref), channel_id=1, source_target_pairs={{0,4},{4,0},{8,12},{12,8},{16,20},{20,16},{24,28},{28,24},{1,5},{5... | collective-permute-start | bytes 6291464 | tf_op jit(solution)/shard_map/ppermute | solution.py:337
  115.5 11.9 %copy-start.16 = (bf16[2048,512]{1,0:T(8,128)(2,1)S(1)}, bf16[2048,512]{1,0:T(8,128)(2,1)}, u32[]{:S(2)}) copy-start(bf16[2048,512]{1,0:T(8,128)(2,1)} %copy-done.15) | copy-start | bytes 6291460
  125.2 26.2 %collective-permute-start.1 = (bf16[1040,512]{1,0:T(8,128)(2,1)S(1)}, bf16[1040,512]{1,0:T(8,128)(2,1)S(1)}, u32[]{:S(2)}, u32[]{:S(2)}) collective-permute-start(bf16[1040,512]{1,0:T(8,128)(2,1)S(1)} %get-tuple-element.23.mine_ref), channel_id=1, source_target_pairs={{0,8},{4,12},{8,0},{12,4},{16,24},{20,28},{24,16},{28,20},{1,9},{5... | collective-permute-start | bytes 3194888 | tf_op jit(solution)/shard_map/ppermute | solution.py:337
  133.0 19.6 %copy-start.11 = (bf16[2048,512]{1,0:T(8,128)(2,1)}, bf16[2048,512]{1,0:T(8,128)(2,1)S(1)}, u32[]{:S(2)}) copy-start(bf16[2048,512]{1,0:T(8,128)(2,1)S(1)} %shard_map.149.base_ref) | copy-start | bytes 6291460
  152.6 2.7 %collective-permute-start.2 = (bf16[1040,512]{1,0:T(8,128)(2,1)S(1)}, bf16[1040,512]{1,0:T(8,128)(2,1)S(1)}, u32[]{:S(2)}, u32[]{:S(2)}) collective-permute-start(bf16[1040,512]{1,0:T(8,128)(2,1)S(1)} %shard_map.150.mine_ref.refs_0_), channel_id=1, source_target_pairs={{0,4},{4,0},{8,12},{12,8},{16,20},{20,16},{24,28},{28,24},{1,5},{5... | collective-permute-start | bytes 3194888 | tf_op jit(solution)/shard_map/ppermute | solution.py:337
  158.3 1.6 copy-start.12
  165.6 1.3 copy-start.13
  204.0 1.6 copy-start
  205.6 16.5 %copy-start.14 = (bf16[2048,512]{1,0:T(8,128)(2,1)S(1)}, bf16[2048,512]{1,0:T(8,128)(2,1)}, u32[]{:S(2)}) copy-start(bf16[2048,512]{1,0:T(8,128)(2,1)} %copy-done.13) | copy-start | bytes 6291460
  206.5 13.7 %collective-permute-start.3 = (bf16[512,512]{1,0:T(8,128)(2,1)S(1)}, bf16[512,512]{1,0:T(8,128)(2,1)S(1)}, u32[]{:S(2)}, u32[]{:S(2)}) collective-permute-start(bf16[512,512]{1,0:T(8,128)(2,1)S(1)} %shard_map.153.refs_0_), channel_id=1, source_target_pairs={{0,8},{4,12},{8,0},{12,4},{16,24},{20,28},{24,16},{28,20},{1,9},{5... | collective-permute-start | bytes 1572872 | tf_op jit(solution)/shard_map/ppermute | solution.py:337
  208.0 12.2 %collective-permute-start.4 = (bf16[512,512]{1,0:T(8,128)(2,1)S(1)}, bf16[512,512]{1,0:T(8,128)(2,1)S(1)}, u32[]{:S(2)}, u32[]{:S(2)}) collective-permute-start(bf16[512,512]{1,0:T(8,128)(2,1)S(1)} %shard_map.153.refs_0_), channel_id=1, source_target_pairs={{0,4},{4,0},{8,12},{12,8},{16,20},{20,16},{24,28},{28,24},{1,5},{5... | collective-permute-start | bytes 1572872 | tf_op jit(solution)/shard_map/ppermute | solution.py:337
  220.2 1.9 collective-permute-start.5
Sparse Core Ops, SparseCore 0:
  158.5 45.5 all-gather.2

commit v3 on v1

--- a/solution.py
+++ b/solution.py
@@ -210,7 +210,9 @@
     per = features // LANES
     lines = []
     for c in range(0, len(columns), per):
-        lines.append(jnp.concatenate([col.T[0:1, :] for col in columns[c : c + per]], axis=1))
+        parts = [col.T[0:1, :] for col in columns[c : c + per]]
+        parts += [jnp.zeros((1, LANES), f32)] * (per - len(parts))
+        lines.append(jnp.concatenate(parts, axis=1))
     which = rows_of((PAD, features))
     tail = jnp.zeros((PAD, features), f32)
     for i, line in enumerate(lines):
@@ -273,7 +275,7 @@
     put_counts(out_ref, count, columns)
 
 
-def pick_kernel(place_ref, pick_ref, mine_ref, other_ref, out_ref, wide):
+def pick_kernel(groups, place_ref, pick_ref, mine_ref, other_ref, out_ref, wide):
     count = mine_ref.shape[0] - PAD
     features = out_ref.shape[1]
     picked = pick_ref.shape[1]
@@ -288,26 +290,91 @@
             )
     sel = picker(pick_ref, 0, picked, 0, 2 * count)
     got = dot(sel, wide[...])
-    out_ref[0:picked, :] = got[:, 0:features].astype(bf16)
-    put_counts(
-        out_ref,
-        picked,
-        [got[c : c + LANES, features : features + LANES] for c in range(0, picked, LANES)],
-    )
-
-
-def three_kernel(all_ref, weight_ref, out_ref):
-    groups = all_ref.shape[0]
-    count, features = out_ref.shape
-    tails = [all_ref[g, count : count + PAD, :].astype(f32) for g in range(groups)]
-    for c in range(0, count, LANES):
+    piece = picked // groups
+    for g in range(groups):
+        base, first = g * (piece + PAD), g * piece
+        out_ref[base : base + piece, :] = got[first : first + piece, 0:features].astype(bf16)
+        columns = [
+            got[first + c : first + c + LANES, features : features + LANES]
+            for c in range(0, piece, LANES)
+        ]
+        put_counts(out_ref, base + piece, columns)
+
+
+def top_kernel(groups, parts_ref, weight_ref, level_ref, inbox, sends, receives):
+    packet = parts_ref.shape[0] // groups
+    piece = packet - PAD
+    features = level_ref.shape[1]
+    a, g = lax.axis_index("sub"), lax.axis_index("grp")
+    across = a + 2 - 4 * ((a // 2) % 2)
+    core = a + 1 - 2 * (a % 2)
+    others = [lax.rem(g + d, groups) for d in range(1, groups)]
+    peers = [{"grp": t} for t in others] + [{"sub": across}, {"sub": core}]
+    barrier = pltpu.get_barrier_semaphore()
+    for peer in peers:
+        pl.semaphore_signal(barrier, inc=1, device_id=peer, device_id_type=pl.DeviceIdType.MESH)
+    pl.semaphore_wait(barrier, len(peers))
+
+    def packet_of(t):
+        return pl.ds(pl.multiple_of(t * packet, PAD), packet)
+
+    def piece_of(sub, group):
+        return pl.ds(pl.multiple_of(((sub % 4) * groups + group) * piece, piece), piece)
+
+    def send(stage, d, source, target, peer):
+        copy = pltpu.make_async_remote_copy(
+            src_ref=source,
+            dst_ref=target,
+            send_sem=sends.at[stage, d],
+            recv_sem=receives.at[stage, d],
+            device_id=peer,
+            device_id_type=pl.DeviceIdType.MESH,
+        )
+        copy.start()
+        return copy
+
+    def relay(stage, d, rows, peer):
+        return send(stage, d, level_ref.at[rows, :], level_ref.at[rows, :], peer)
+
+    first = [
+        send(0, d, parts_ref.at[packet_of(t), :], inbox.at[d], {"grp": t})
+        for d, t in enumerate(others)
+    ]
+    own = pl.multiple_of(g * packet, PAD)
+    for copy in first:
+        copy.wait_recv()
+    terms = [lambda at, size: parts_ref[pl.ds(own + at, size), :].astype(f32)]
+    for d in range(groups - 1):
+        terms.append(lambda at, size, d=d: inbox[d, at : at + size, :].astype(f32))
+    tails = [term(piece, PAD) for term in terms]
+    base = pl.multiple_of(((a % 4) * groups + g) * piece, piece)
+    for c in range(0, piece, LANES):
         total, marks = 0.0, 0.0
-        for g in range(groups):
-            got = get_count(tails[g], c)
+        for term, tail in zip(terms, tails):
+            got = get_count(tail, c)
             marks = marks + got
-            total = total + widened(got, features) * all_ref[g, c : c + LANES, :].astype(f32)
+            total = total + widened(got, features) * term(c, LANES)
         level = refined(total, widened(marks, features), weight_ref[...])
-        out_ref[c : c + LANES, :] = level.astype(bf16)
+        level_ref[pl.ds(base + c, LANES), :] = level.astype(bf16)
+
+    mine = piece_of(a, g)
+    pieces = [mine] + [piece_of(a, lax.rem(g + groups - d, groups)) for d in range(1, groups)]
+    theirs = [piece_of(across, lax.rem(g + groups - d, groups)) for d in range(groups)]
+    over_x = [relay(2, 0, mine, {"sub": across})]
+    over_z = [relay(1, d, mine, {"grp": t}) for d, t in enumerate(others)]
+    over_core = [relay(3, 0, mine, {"sub": core})]
+    for d in range(1, groups):
+        over_z[d - 1].wait_recv()
+        over_x.append(relay(2, d, pieces[d], {"sub": across}))
+        over_core.append(relay(3, d, pieces[d], {"sub": core}))
+    relayed = []
+    for d in range(groups):
+        over_x[d].wait_recv()
+        relayed.append(relay(4, d, theirs[d], {"sub": core}))
+    for copy in over_core + relayed:
+        copy.wait_recv()
+    for copy in first + over_z + over_x + over_core + relayed:
+        copy.wait_send()
 
 
 def back_kernel(last, order, place_ref, perm_ref, base_ref, *refs):
@@ -390,6 +457,7 @@
         scratch=[pltpu.VMEM((8, slot_rows), f32), pltpu.VMEM((8, slot_rows), f32)],
         flops=20 * 10**9,
     )
+    arrived, to_two, to_three = lax.optimization_barrier((arrived, to_two, to_three))
 
     fine, side = call(
         fine_kernel,
@@ -434,17 +502,31 @@
         specs=[SM] + [VM] * 3,
         flops=wide_flops,
     )
+    other, raised = lax.optimization_barrier((other, raised))
     mine = call(two_kernel, shape(half + PAD), (mine, other, coarse[1]), flops=10**9)
     other = swapped(mine, 1)
+    groups = lax.axis_size("grp")
+    packet = quarter // groups + PAD
     chosen = call(
-        pick_kernel,
-        shape(quarter + PAD),
+        functools.partial(pick_kernel, groups),
+        shape(groups * packet),
         (place, top_quarter, mine, other),
         specs=[SM] + [VM] * 3,
         scratch=[wide],
         flops=10**9,
     )
-    gathered = lax.all_gather(chosen, "grp", axis=0, tiled=False)
+    level_three = pl.pallas_call(
+        functools.partial(top_kernel, groups),
+        out_shape=shape(slot_rows),
+        in_specs=[VM] * 2,
+        out_specs=VM,
+        scratch_shapes=[
+            pltpu.VMEM((groups - 1, packet, features), bf16),
+            pltpu.SemaphoreType.DMA((5, groups)),
+            pltpu.SemaphoreType.DMA((5, groups)),
+        ],
+        compiler_params=pltpu.CompilerParams(collective_id=0, has_side_effects=True),
+    )(chosen, coarse[2])
     raised = call(
         functools.partial(back, (0, 1)),
         shape(slot_rows),
@@ -452,13 +534,11 @@
         specs=[SM] + [VM] * 4,
         flops=wide_flops,
     )
-    mine = call(three_kernel, shape(quarter), (gathered, coarse[2]), flops=10**9)
-    across = swapped(mine, 2)
     return call(
-        functools.partial(back_kernel, True, (0, 2, 1, 3)),
+        functools.partial(back_kernel, True, (0,)),
         shape(slot_rows),
-        (place, to_three, raised, mine, across, swapped(mine, 1), swapped(across, 1)),
-        specs=[SM] + [VM] * 6,
+        (place, to_three, raised, level_three),
+        specs=[SM] + [VM] * 3,
         flops=wide_flops,
     )
 

time: 247 us -> 206 us (0.83)
  waiting for transfers between devices: 130 us -> 64 us
  Pallas kernels: 82.1 us -> 114 us
  between operations: 13.7 us -> 0.24 us
  local copies, waits for them, and re-layouts: 9.05 us -> 15.7 us
    all_gather x1 -> x0, waiting for transfers between devices: 45.6 us -> none  [body(): gathered = lax.all_gather(chosen, 'grp', axis=0, tiled=False)]
    pallas_call x0 -> x1, Pallas kernels: none -> 35.6 us  [body(): pl.pallas_call(functools.partial(top_kernel, groups), out_shape=shape(slo...]
    ppermute x6 -> x3, waiting for transfers between devices: 37.2 us -> 21.8 us  [swapped(): return lax.ppermute(shard, 'sub', [(i, i ^ flip) for i in range(count)])]
    all_to_all x1, waiting for transfers between devices: 47 us -> 42.2 us  [body(): lax.all_to_all(placed.reshape(owner_count, cap, features), ('sub', 'grp')...]
    unnamed x39 -> x41, local copies, waits for them, and re-layouts: 7.33 us -> 11.9 us
    pallas_call x10 -> x9, Pallas kernels: 82.1 us -> 78.4 us  [call(): pl.pallas_call(kernel, out_shape=outs, in_specs=specs or [VM] * len(args)...]
  transfers between devices with their start and end apart: 8 -> 4, of which waited for: 6 -> 4; matrix products, arithmetic and copies ran while one was open for 1% -> 2% of each run, Pallas kernels for 6% -> 5%
where the time goes in v3:
time: 206 us; the launch traced here: 204 us
  Pallas kernels  114 us (55%)
  waiting for transfers between devices  64 us (31%)
  local copies, waits for them, and re-layouts  15.7 us (8%)
  starting transfers between devices  10.6 us (5%)
    pallas_call x9, Pallas kernels, call(): pl.pallas_call(kernel, out_shape=outs, in_specs=specs or [VM] * len(args)...  78.4 us
    all_to_all x1, waiting for transfers between devices, body(): lax.all_to_all(placed.reshape(owner_count, cap, features), ('sub', 'grp')...  42.2 us
    pallas_call x1, Pallas kernels, body(): pl.pallas_call(functools.partial(top_kernel, groups), out_shape=shape(slo...  35.6 us
    ppermute x3, waiting for transfers between devices, swapped(): return lax.ppermute(shard, 'sub', [(i, i ^ flip) for i in range(count)])  21.8 us
    unnamed x41, local copies, waits for them, and re-layouts  11.9 us
    all_to_all x1, starting transfers between devices, body(): lax.all_to_all(placed.reshape(owner_count, cap, features), ('sub', 'grp')...  7.3 us
  transfers between devices with their start and end apart: 4, of which 4 were waited for; matrix products, arithmetic and copies ran while one was open for 2% of the time, Pallas kernels for 5%

profile of v3, /device:TPU:0, one launch (start us, length us, event | category | flops | bytes accessed | tf_op | source)
XLA Modules:
  0.0 204.5 jit_solution(11716459242751927118)
XLA Ops:
  0.0 1.2 copy-done.2
  1.2 0.7 copy-done.8
  1.9 5.4 %shard_map.145 = bf16[2048,512]{1,0:T(8,128)(2,1)} custom-call(s32[1,1024]{1,0:T(1,128)S(1)} %bitcast.28, bf16[1024,512]{1,0:T(8,128)(2,1)S(1)} %copy-done.2), custom_call_target="tpu_custom_call" | custom-call | flops 2147483648 | bytes 8388608 | tf_op jit(solution)/shard_map/pallas_call | solution.py:27
  7.3 7.3 %all-to-all-start = ((bf16[32,64,512]{2,1,0:T(8,128)(2,1)}), bf16[32,64,512]{2,1,0:T(8,128)(2,1)S(1)}, u32[]{:S(2)}, u32[]{:S(2)}) async-start(bf16[32,64,512]{2,1,0:T(8,128)(2,1)} %bitcast.2), calls=%async_computation | async-start | bytes 4194304 | tf_op jit(solution)/shard_map/all_to_all | solution.py:439
  14.7 0.1 copy.17.tile_ref
  14.8 0.3 copy.16
  15.1 0.7 dynamic-slice_bitcast_fusion
  15.9 4.1 %shard_map.146 = (s32[1,2048]{1,0:T(1,128)S(1)}, s32[1,2048]{1,0:T(1,128)S(1)}) custom-call(s32[1,2048]{1,0:T(1,128)S(1)} %bitcast.25, s32[1,2048]{1,0:T(1,128)S(1)} %get-tuple-element.31.quad_ref, s32[1,2048]{1,0:T(1,128)S(1)} %get-tuple-element.30.top_ref), custom_call_target="tpu_custom_call" | custom-call | flops 20000000000 | bytes 8388608 | tf_op jit(solution)/shard_map/pallas_call | solution.py:27
  20.0 42.2 %all-to-all-done = bf16[32,64,512]{2,1,0:T(8,128)(2,1)S(1)} async-done(((bf16[32,64,512]{2,1,0:T(8,128)(2,1)}), bf16[32,64,512]{2,1,0:T(8,128)(2,1)S(1)}, u32[]{:S(2)}, u32[]{:S(2)}) %all-to-all-start) | async-done | bytes 2097184 | tf_op jit(solution)/shard_map/all_to_all | solution.py:439
  62.2 1.3 copy-done.16
  63.5 1.2 copy-done.3
  64.7 1.2 copy-done.4
  66.0 1.0 copy-done.5
  67.0 1.0 copy-done.6
  68.0 38.0 %shard_map.147 = (bf16[2048,512]{1,0:T(8,128)(2,1)S(1)}, bf16[2048,512]{1,0:T(8,128)(2,1)S(1)}) custom-call(s32[16,2]{1,0:T(8,128)S(1)} %copy.17.tile_ref, bf16[2048,512]{1,0:T(8,128)(2,1)} %bitcast.32, s32[2048,16]{1,0:T(8,128)S(1)} %bitcast.24, s32[1,2048]{1,0:T(1,128)S(1)} %bitcast.26, bf16[2,512,512]{2,1,0:T(8,128)(2,1)S(1)} %copy-done.3, ...), custom_call_target="tpu_custom_call" | custom-call | flops 40000000000 | bytes 8388608 | tf_op jit(solution)/shard_map/pallas_call | solution.py:27
  106.1 1.3 copy-done.14
  107.4 1.0 collective-permute-start
  108.4 0.8 dynamic-slice_bitcast_fusion.2.pick_ref
  109.2 2.2 %slice_bitcast_fusion = (bf16[512,512]{1,0:T(8,128)(2,1)}, bf16[512,512]{1,0:T(8,128)(2,1)S(1)}, bf16[512,512]{1,0:T(8,128)(2,1)S(1)}) fusion(bf16[3,512,512]{2,1,0:T(8,128)(2,1)} %param.29), kind=kLoop, calls=%fused_computation | loop fusion | bytes 3145728 | tf_op jit(solution)/shard_map/squeeze | solution.py:529
  111.4 0.9 collective-permute-done.other_ref
  112.3 9.1 %shard_map.148 = (bf16[2048,512]{1,0:T(8,128)(2,1)S(1)}, bf16[1040,512]{1,0:T(8,128)(2,1)S(1)}) custom-call(s32[1,1024]{1,0:T(1,128)S(1)} %dynamic-slice_bitcast_fusion.2.pick_ref, bf16[2048,512]{1,0:T(8,128)(2,1)S(1)} %get-tuple-element.21.side_ref, bf16[2048,512]{1,0:T(8,128)(2,1)} %collective-permute-done.other_ref, ...), custom_call_target="tpu_custom_call" | custom-call | flops 4000000000 | bytes 8388608 | tf_op jit(solution)/shard_map/pallas_call | solution.py:27
  121.4 2.2 %collective-permute-start.1 = (bf16[1040,512]{1,0:T(8,128)(2,1)S(1)}, bf16[1040,512]{1,0:T(8,128)(2,1)S(1)}, u32[]{:S(2)}, u32[]{:S(2)}) collective-permute-start(bf16[1040,512]{1,0:T(8,128)(2,1)S(1)} %get-tuple-element.22.mine_ref), channel_id=1, source_target_pairs={{0,8},{4,12},{8,0},{12,4},{16,24},{20,28},{24,16},{28,20},{1,9},{5... | collective-permute-start | bytes 3194888 | tf_op jit(solution)/shard_map/ppermute | solution.py:403
  123.6 5.7 %shard_map.149.base_ref = bf16[2048,512]{1,0:T(8,128)(2,1)S(1)} custom-call(s32[1]{0:T(128)} %bitcast.place_ref, s32[1,2048]{1,0:T(1,128)S(1)} %bitcast.27, bf16[2048,512]{1,0:T(8,128)(2,1)S(1)} %copy-done.15, bf16[2048,512]{1,0:T(8,128)(2,1)S(1)} %get-tuple-element.24.refs_0_), custom_call_target="tpu_custom_call" | custom-call | flops 4294967296 | bytes 8388608 | tf_op jit(solution)/shard_map/pallas_call | solution.py:27
  129.3 18.3 %collective-permute-done.1.other_ref = bf16[1040,512]{1,0:T(8,128)(2,1)S(1)} collective-permute-done((bf16[1040,512]{1,0:T(8,128)(2,1)S(1)}, bf16[1040,512]{1,0:T(8,128)(2,1)S(1)}, u32[]{:S(2)}, u32[]{:S(2)}) %collective-permute-start.1) | collective-permute-done | bytes 1064992 | tf_op jit(solution)/shard_map/ppermute | solution.py:403
  147.7 1.2 shard_map.150.refs_0_.mine_ref
  149.1 2.6 %collective-permute-done.2.refs_1_.other_ref = bf16[1040,512]{1,0:T(8,128)(2,1)S(1)} collective-permute-done((bf16[1040,512]{1,0:T(8,128)(2,1)S(1)}, bf16[1040,512]{1,0:T(8,128)(2,1)S(1)}, u32[]{:S(2)}, u32[]{:S(2)}) %collective-permute-start.2) | collective-permute-done | bytes 1064992 | tf_op jit(solution)/shard_map/ppermute | solution.py:403
  151.7 2.1 %shard_map.152.parts_ref = bf16[576,512]{1,0:T(8,128)(2,1)S(1)} custom-call(s32[1]{0:T(128)} %bitcast.place_ref, s32[1,512]{1,0:T(1,128)S(1)} %dynamic-slice_bitcast_fusion.3.pick_ref, bf16[1040,512]{1,0:T(8,128)(2,1)S(1)} %shard_map.150.refs_0_.mine_ref, bf16[1040,512]{1,0:T(8,128)(2,1)S(1)} %collective-permute-done.2.refs_1_.other_ref), custom_call_target="tpu_custom_call" | custom-call | flops 1000000000 | bytes 8388608 | tf_op jit(solution)/shard_map/pallas_call | solution.py:27
  153.8 0.8 copy-done.1
  154.6 35.6 %shard_map.153.refs_0_ = bf16[2048,512]{1,0:T(8,128)(2,1)} custom-call(bf16[576,512]{1,0:T(8,128)(2,1)} %copy-done.1, bf16[512,512]{1,0:T(8,128)(2,1)} %get-tuple-element.27.weight_ref), custom_call_target="tpu_custom_call" | custom-call | tf_op jit(solution)/shard_map/pallas_call | solution.py:518
  190.2 1.6 copy-done.13
  191.8 5.7 %shard_map.151.base_ref = bf16[2048,512]{1,0:T(8,128)(2,1)S(1)} custom-call(s32[1]{0:T(128)} %bitcast.place_ref, s32[1,2048]{1,0:T(1,128)S(1)} %get-tuple-element.19.perm_ref, bf16[2048,512]{1,0:T(8,128)(2,1)S(1)} %copy-done.13, bf16[1040,512]{1,0:T(8,128)(2,1)S(1)} %shard_map.150.refs_0_.mine_ref, bf16[1040,512]{1,0:T(8,128)(2,1)S(1)} %collective-permute-done.2.refs_1_.other_ref), custom_call_target="tpu_custom_call" | custom-call | flops 4294967296 | bytes 8388608 | tf_op jit(solution)/shard_map/pallas_call | solution.py:27
  197.5 7.0 %shard_map.154 = bf16[2048,512]{1,0:T(8,128)(2,1)} custom-call(s32[1]{0:T(128)} %bitcast.place_ref, s32[1,2048]{1,0:T(1,128)S(1)} %get-tuple-element.18.perm_ref, bf16[2048,512]{1,0:T(8,128)(2,1)S(1)} %shard_map.151.base_ref, bf16[2048,512]{1,0:T(8,128)(2,1)S(1)} %copy-done), custom_call_target="tpu_custom_call" | custom-call | flops 4294967296 | bytes 8388608 | tf_op jit(solution)/shard_map/pallas_call | solution.py:27
  (32 shorter events, 0.2 us)
Async XLA Ops:
  0.0 1.2 copy-start.2
  1.2 0.7 copy-start.8
  7.3 7.4 %copy-start.19 = (s32[1,1,16,2]{2,3,1,0:T(2,128)S(1)}, s32[1,1,16,2]{2,3,1,0:T(2,128)}, u32[]{:S(2)}) copy-start(s32[1,1,16,2]{2,3,1,0:T(2,128)} %param.17) | copy-start | bytes 388
  7.3 7.5 %copy-start.17 = (s32[1,1,2048,16]{2,3,1,0:T(8,128)S(1)}, s32[1,1,2048,16]{2,3,1,0:T(8,128)}, u32[]{:S(2)}) copy-start(s32[1,1,2048,16]{2,3,1,0:T(8,128)} %param.18) | copy-start | bytes 393220
  7.3 7.8 %copy-start.18 = (s32[2,1,2048]{2,1,0:T(1,128)S(1)}, s32[2,1,2048]{2,1,0:T(1,128)}, u32[]{:S(2)}) copy-start(s32[2,1,2048]{2,1,0:T(1,128)} %param.21) | copy-start | bytes 49156
  7.3 8.5 %copy-start.7 = (s32[1,1,2048]{2,1,0:T(1,128)S(1)}, s32[1,1,2048]{2,1,0:T(1,128)}, u32[]{:S(2)}) copy-start(s32[1,1,2048]{2,1,0:T(1,128)} %param.19) | copy-start | bytes 24580
  7.3 54.8 %all-to-all-start = ((bf16[32,64,512]{2,1,0:T(8,128)(2,1)}), bf16[32,64,512]{2,1,0:T(8,128)(2,1)S(1)}, u32[]{:S(2)}, u32[]{:S(2)}) async-start(bf16[32,64,512]{2,1,0:T(8,128)(2,1)} %bitcast.2), calls=%async_computation | async-start | bytes 4194304 | tf_op jit(solution)/shard_map/all_to_all | solution.py:439
  15.9 47.6 %copy-start.9 = (f32[512]{0:T(512)S(1)}, f32[512]{0:T(512)}, u32[]{:S(2)}) copy-start(f32[512]{0:T(512)} %param.23) | copy-start | bytes 6148
  15.9 47.6 %copy-start.10 = (f32[512]{0:T(512)S(1)}, f32[512]{0:T(512)}, u32[]{:S(2)}) copy-start(f32[512]{0:T(512)} %param.26) | copy-start | bytes 6148
  15.9 47.6 %copy-start.11 = (f32[512]{0:T(512)S(1)}, f32[512]{0:T(512)}, u32[]{:S(2)}) copy-start(f32[512]{0:T(512)} %param.28) | copy-start | bytes 6148
  62.2 1.3 copy-start.16
  63.5 1.2 copy-start.3
  64.7 1.2 copy-start.4
  66.0 1.0 copy-start.5
  67.0 1.0 copy-start.6
  106.1 1.3 copy-start.14
  107.4 4.9 %collective-permute-start = (bf16[2048,512]{1,0:T(8,128)(2,1)S(1)}, bf16[2048,512]{1,0:T(8,128)(2,1)}, u32[]{:S(2)}, u32[]{:S(2)}) collective-permute-start(bf16[2048,512]{1,0:T(8,128)(2,1)S(1)} %get-tuple-element.21.side_ref), channel_id=1, source_target_pairs={{0,4},{4,0},{8,12},{12,8},{16,20},{20,16},{24,28},{28,24},{1,5},{5... | collective-permute-start | bytes 6291464 | tf_op jit(solution)/shard_map/ppermute | solution.py:403
  112.3 11.3 %copy-start.15 = (bf16[2048,512]{1,0:T(8,128)(2,1)S(1)}, bf16[2048,512]{1,0:T(8,128)(2,1)}, u32[]{:S(2)}) copy-start(bf16[2048,512]{1,0:T(8,128)(2,1)} %copy-done.14) | copy-start | bytes 6291460
  121.4 26.2 %collective-permute-start.1 = (bf16[1040,512]{1,0:T(8,128)(2,1)S(1)}, bf16[1040,512]{1,0:T(8,128)(2,1)S(1)}, u32[]{:S(2)}, u32[]{:S(2)}) collective-permute-start(bf16[1040,512]{1,0:T(8,128)(2,1)S(1)} %get-tuple-element.22.mine_ref), channel_id=1, source_target_pairs={{0,8},{4,12},{8,0},{12,4},{16,24},{20,28},{24,16},{28,20},{1,9},{5... | collective-permute-start | bytes 3194888 | tf_op jit(solution)/shard_map/ppermute | solution.py:403
  129.3 19.6 %copy-start.12 = (bf16[2048,512]{1,0:T(8,128)(2,1)}, bf16[2048,512]{1,0:T(8,128)(2,1)S(1)}, u32[]{:S(2)}) copy-start(bf16[2048,512]{1,0:T(8,128)(2,1)S(1)} %shard_map.149.base_ref) | copy-start | bytes 6291460
  148.9 2.7 %collective-permute-start.2 = (bf16[1040,512]{1,0:T(8,128)(2,1)S(1)}, bf16[1040,512]{1,0:T(8,128)(2,1)S(1)}, u32[]{:S(2)}, u32[]{:S(2)}) collective-permute-start(bf16[1040,512]{1,0:T(8,128)(2,1)S(1)} %shard_map.150.refs_0_.mine_ref), channel_id=1, source_target_pairs={{0,4},{4,0},{8,12},{12,8},{16,20},{20,16},{24,28},{28,24},{1,5},{5... | collective-permute-start | bytes 3194888 | tf_op jit(solution)/shard_map/ppermute | solution.py:403
  153.8 0.8 copy-start.1
  190.2 1.6 copy-start.13
  191.8 5.7 %copy-start = (bf16[2048,512]{1,0:T(8,128)(2,1)S(1)}, bf16[2048,512]{1,0:T(8,128)(2,1)}, u32[]{:S(2)}) copy-start(bf16[2048,512]{1,0:T(8,128)(2,1)} %shard_map.153.refs_0_) | copy-start | bytes 6291460

commit v4 on v3

--- a/solution.py
+++ b/solution.py
@@ -133,8 +133,10 @@
     dst,
     src,
     agg,
-    sels,
-    near_rows,
+    sels_a,
+    sels_b,
+    near_a,
+    near_b,
 ):
     count, features = fine_ref.shape
     tile = 256
@@ -152,26 +154,36 @@
         src[here, :] = jnp.where(present, from_src, AWAY).astype(bf16)
 
     group = 16
-
-    @pl.loop(0, count // BLK)
-    def _(b):
-        start = pl.multiple_of(b * BLK, BLK)
-        near = near_ref[pl.ds(start, BLK), :]
+    blocks = count // BLK
+
+    def gather(b, sels, near_rows):
+        near = near_ref[pl.ds(pl.multiple_of(b * BLK, BLK), BLK), :]
         for j in range(TPB):
+            first = pl.multiple_of(tile_ref[b, j] * BLK, BLK)
             for k in range(NBR):
                 at = j * NBR + k
                 mask = near[:, at : at + 1] == lanes_of((BLK, BLK))
-                sels[k * BLK : (k + 1) * BLK, :] = one_hot(mask)
-            first = pl.multiple_of(tile_ref[b, j] * BLK, BLK)
-            near_rows[j * NBR * BLK : (j + 1) * NBR * BLK, :] = dot(
-                sels[...], src[pl.ds(first, BLK), :]
-            )
+                sels[at * BLK : (at + 1) * BLK, :] = one_hot(mask)
+            part = slice(j * NBR * BLK, (j + 1) * NBR * BLK)
+            near_rows[part, :] = dot(sels[part, :], src[pl.ds(first, BLK), :])
+
+    def sum_edges(b, near_rows):
+        start = pl.multiple_of(b * BLK, BLK)
         for r in range(0, BLK, group):
             here = dst[pl.ds(start + r, group), :].astype(f32)
             total = jnp.zeros((group, features), f32)
             for at in range(TPB * NBR):
                 total += half_silu(here + near_rows[at * BLK + r : at * BLK + r + group, :])
             agg[pl.ds(start + r, group), :] = total.astype(bf16)
+
+    gather(0, sels_a, near_a)
+
+    @pl.loop(0, blocks // 2)
+    def _(i):
+        gather(2 * i + 1, sels_b, near_b)
+        sum_edges(2 * i, near_a)
+        gather(jnp.minimum(2 * i + 2, blocks - 1), sels_a, near_a)
+        sum_edges(2 * i + 1, near_b)
 
     @pl.loop(0, count // tile)
     def _(t):
@@ -377,10 +389,13 @@
         copy.wait_send()
 
 
-def back_kernel(last, order, place_ref, perm_ref, base_ref, *refs):
-    pieces, out_ref = refs[:-1], refs[-1]
-    width = perm_ref.shape[1]
-    size = width // len(pieces)
+def sent(perm_ref, first, rows, start, tile):
+    size = rows.shape[0]
+    targets = perm_ref[:, pl.ds(first, size)]
+    return dot(one_hot(rows_of((tile, size), start) == targets), rows)
+
+
+def back_kernel(perm_ref, base_ref, level_ref, out_ref):
     tile = 256
 
     @pl.loop(0, out_ref.shape[0] // tile)
@@ -388,14 +403,28 @@
         start = pl.multiple_of(t * tile, tile)
         here = pl.ds(start, tile)
         base = base_ref[here, :].astype(f32)
-        total = base
-        for piece, flip in zip(pieces, order):
-            at = (place_ref[0] % len(pieces)) ^ flip
-            targets = perm_ref[:, pl.ds(pl.multiple_of(at * size, LANES), size)]
-            sel = one_hot(rows_of((tile, size), start) == targets)
-            total = total + dot(sel, piece[0:size, :])
-        absent = 0.0 if last else EMPTY
-        out_ref[here, :] = jnp.where(base[:, 0:1] < LIMIT, total, absent).astype(bf16)
+        total = base + sent(perm_ref, 0, level_ref[...], start, tile)
+        out_ref[here, :] = jnp.where(base[:, 0:1] < LIMIT, total, EMPTY).astype(bf16)
+
+
+def last_kernel(
+    place_ref, two_ref, three_ref, base_ref, mine_ref, other_ref, level_ref, out_ref
+):
+    tile = 256
+    half = level_ref.shape[0] // 2
+    core = place_ref[0] % 2
+    mine_at = pl.multiple_of(core * half, LANES)
+    other_at = pl.multiple_of((1 - core) * half, LANES)
+
+    @pl.loop(0, out_ref.shape[0] // tile)
+    def _(t):
+        start = pl.multiple_of(t * tile, tile)
+        here = pl.ds(start, tile)
+        base = base_ref[here, :].astype(f32)
+        total = base + sent(three_ref, 0, level_ref[...], start, tile)
+        total += sent(two_ref, mine_at, mine_ref[0:half, :], start, tile)
+        total += sent(two_ref, other_at, other_ref[0:half, :], start, tile)
+        out_ref[here, :] = jnp.where(base[:, 0:1] < LIMIT, total, 0.0).astype(bf16)
 
 
 def swapped(shard, flip):
@@ -478,7 +507,9 @@
         specs=[SM] + [VM] * 10,
         scratch=[pltpu.VMEM((slot_rows, features), bf16)] * 4
         + [
-            pltpu.VMEM((NBR * BLK, BLK), bf16),
+            pltpu.VMEM((TPB * NBR * BLK, BLK), bf16),
+            pltpu.VMEM((TPB * NBR * BLK, BLK), bf16),
+            pltpu.VMEM((TPB * NBR * BLK, features), f32),
             pltpu.VMEM((TPB * NBR * BLK, features), f32),
         ],
         flops=40 * 10**9,
@@ -493,14 +524,9 @@
         flops=4 * 10**9,
     )
     other = swapped(mine, 2)
-    back = functools.partial(back_kernel, False)
     wide_flops = 2 * slot_rows * slot_rows * features
     raised = call(
-        functools.partial(back, (0,)),
-        shape(slot_rows),
-        (place, pair, fine, level_one),
-        specs=[SM] + [VM] * 3,
-        flops=wide_flops,
+        back_kernel, shape(slot_rows), (pair, fine, level_one), flops=wide_flops
     )
     other, raised = lax.optimization_barrier((other, raised))
     mine = call(two_kernel, shape(half + PAD), (mine, other, coarse[1]), flops=10**9)
@@ -527,19 +553,12 @@
         ],
         compiler_params=pltpu.CompilerParams(collective_id=0, has_side_effects=True),
     )(chosen, coarse[2])
-    raised = call(
-        functools.partial(back, (0, 1)),
+    return call(
+        last_kernel,
         shape(slot_rows),
-        (place, to_two, raised, mine, other),
-        specs=[SM] + [VM] * 4,
-        flops=wide_flops,
-    )
-    return call(
-        functools.partial(back_kernel, True, (0,)),
-        shape(slot_rows),
-        (place, to_three, raised, level_three),
-        specs=[SM] + [VM] * 3,
-        flops=wide_flops,
+        (place, to_two, to_three, raised, mine, other, level_three),
+        specs=[SM] + [VM] * 6,
+        flops=2 * wide_flops,
     )
 
 

time: 206 us -> 208 us (level)
    pallas_call x9 -> x8, Pallas kernels: 78.4 us -> 78.8 us  [call(): pl.pallas_call(kernel, out_shape=outs, in_specs=specs or [VM] * len(args)...]
where the time goes in v4:
time: 208 us; the launch traced here: 206 us
  Pallas kernels  114 us (55%)
  waiting for transfers between devices  63.8 us (31%)
  local copies, waits for them, and re-layouts  17.3 us (8%)
  starting transfers between devices  10.6 us (5%)
    pallas_call x8, Pallas kernels, call(): pl.pallas_call(kernel, out_shape=outs, in_specs=specs or [VM] * len(args)...  78.8 us
    all_to_all x1, waiting for transfers between devices, body(): lax.all_to_all(placed.reshape(owner_count, cap, features), ('sub', 'grp')...  42.2 us
    pallas_call x1, Pallas kernels, body(): pl.pallas_call(functools.partial(top_kernel, groups), out_shape=shape(slo...  35.6 us
    ppermute x3, waiting for transfers between devices, swapped(): return lax.ppermute(shard, 'sub', [(i, i ^ flip) for i in range(count)])  21.6 us
    unnamed x41, local copies, waits for them, and re-layouts  13.4 us
    all_to_all x1, starting transfers between devices, body(): lax.all_to_all(placed.reshape(owner_count, cap, features), ('sub', 'grp')...  7.3 us
  transfers between devices with their start and end apart: 4, of which 4 were waited for; matrix products, arithmetic and copies ran while one was open for 2% of the time, Pallas kernels for 5%

profile of v4, /device:TPU:0, one launch (start us, length us, event | category | flops | bytes accessed | tf_op | source)
XLA Modules:
  0.0 206.3 jit_solution(12640335475583933734)
XLA Ops:
  0.0 1.2 copy-done.2
  1.2 0.7 copy-done.8
  1.9 5.4 %shard_map.145 = bf16[2048,512]{1,0:T(8,128)(2,1)} custom-call(s32[1,1024]{1,0:T(1,128)S(1)} %bitcast.28, bf16[1024,512]{1,0:T(8,128)(2,1)S(1)} %copy-done.2), custom_call_target="tpu_custom_call" | custom-call | flops 2147483648 | bytes 8388608 | tf_op jit(solution)/shard_map/pallas_call | solution.py:27
  7.3 7.3 %all-to-all-start = ((bf16[32,64,512]{2,1,0:T(8,128)(2,1)}), bf16[32,64,512]{2,1,0:T(8,128)(2,1)S(1)}, u32[]{:S(2)}, u32[]{:S(2)}) async-start(bf16[32,64,512]{2,1,0:T(8,128)(2,1)} %bitcast.2), calls=%async_computation | async-start | bytes 4194304 | tf_op jit(solution)/shard_map/all_to_all | solution.py:468
  14.7 0.1 copy.17.tile_ref
  14.8 0.3 copy.16
  15.1 0.7 dynamic-slice_bitcast_fusion
  15.9 4.1 %shard_map.146 = (s32[1,2048]{1,0:T(1,128)S(1)}, s32[1,2048]{1,0:T(1,128)S(1)}) custom-call(s32[1,2048]{1,0:T(1,128)S(1)} %bitcast.25, s32[1,2048]{1,0:T(1,128)S(1)} %get-tuple-element.31.quad_ref, s32[1,2048]{1,0:T(1,128)S(1)} %get-tuple-element.30.top_ref), custom_call_target="tpu_custom_call" | custom-call | flops 20000000000 | bytes 8388608 | tf_op jit(solution)/shard_map/pallas_call | solution.py:27
  20.0 42.2 %all-to-all-done = bf16[32,64,512]{2,1,0:T(8,128)(2,1)S(1)} async-done(((bf16[32,64,512]{2,1,0:T(8,128)(2,1)}), bf16[32,64,512]{2,1,0:T(8,128)(2,1)S(1)}, u32[]{:S(2)}, u32[]{:S(2)}) %all-to-all-start) | async-done | bytes 2097184 | tf_op jit(solution)/shard_map/all_to_all | solution.py:468
  62.2 1.3 copy-done.16
  63.5 1.2 copy-done.3
  64.7 1.2 copy-done.4
  66.0 1.0 copy-done.5
  67.0 1.0 copy-done.6
  68.0 39.7 %shard_map.147 = (bf16[2048,512]{1,0:T(8,128)(2,1)S(1)}, bf16[2048,512]{1,0:T(8,128)(2,1)S(1)}) custom-call(s32[16,2]{1,0:T(8,128)S(1)} %copy.17.tile_ref, bf16[2048,512]{1,0:T(8,128)(2,1)} %bitcast.32, s32[2048,16]{1,0:T(8,128)S(1)} %bitcast.24, s32[1,2048]{1,0:T(1,128)S(1)} %bitcast.26, bf16[2,512,512]{2,1,0:T(8,128)(2,1)S(1)} %copy-done.3, ...), custom_call_target="tpu_custom_call" | custom-call | flops 40000000000 | bytes 8388608 | tf_op jit(solution)/shard_map/pallas_call | solution.py:27
  107.7 1.3 copy-done.14
  109.0 1.0 collective-permute-start
  110.0 0.8 dynamic-slice_bitcast_fusion.2.pick_ref
  110.8 2.2 %slice_bitcast_fusion = (bf16[512,512]{1,0:T(8,128)(2,1)}, bf16[512,512]{1,0:T(8,128)(2,1)S(1)}, bf16[512,512]{1,0:T(8,128)(2,1)S(1)}) fusion(bf16[3,512,512]{2,1,0:T(8,128)(2,1)} %param.29), kind=kLoop, calls=%fused_computation | loop fusion | bytes 3145728 | tf_op jit(solution)/shard_map/squeeze | solution.py:555
  113.0 0.9 collective-permute-done.other_ref
  113.9 9.1 %shard_map.148 = (bf16[2048,512]{1,0:T(8,128)(2,1)S(1)}, bf16[1040,512]{1,0:T(8,128)(2,1)S(1)}) custom-call(s32[1,1024]{1,0:T(1,128)S(1)} %dynamic-slice_bitcast_fusion.2.pick_ref, bf16[2048,512]{1,0:T(8,128)(2,1)S(1)} %get-tuple-element.21.side_ref, bf16[2048,512]{1,0:T(8,128)(2,1)} %collective-permute-done.other_ref, ...), custom_call_target="tpu_custom_call" | custom-call | flops 4000000000 | bytes 8388608 | tf_op jit(solution)/shard_map/pallas_call | solution.py:27
  123.0 2.2 %collective-permute-start.1 = (bf16[1040,512]{1,0:T(8,128)(2,1)S(1)}, bf16[1040,512]{1,0:T(8,128)(2,1)S(1)}, u32[]{:S(2)}, u32[]{:S(2)}) collective-permute-start(bf16[1040,512]{1,0:T(8,128)(2,1)S(1)} %get-tuple-element.22.mine_ref), channel_id=1, source_target_pairs={{0,8},{4,12},{8,0},{12,4},{16,24},{20,28},{24,16},{28,20},{1,9},{5... | collective-permute-start | bytes 3194888 | tf_op jit(solution)/shard_map/ppermute | solution.py:432
  125.3 5.8 %shard_map.149.base_ref = bf16[2048,512]{1,0:T(8,128)(2,1)S(1)} custom-call(s32[1,2048]{1,0:T(1,128)S(1)} %bitcast.27, bf16[2048,512]{1,0:T(8,128)(2,1)S(1)} %copy-done.15, bf16[2048,512]{1,0:T(8,128)(2,1)S(1)} %get-tuple-element.24.level_ref), custom_call_target="tpu_custom_call" | custom-call | flops 4294967296 | bytes 8388608 | tf_op jit(solution)/shard_map/pallas_call | solution.py:27
  131.1 18.2 %collective-permute-done.1.other_ref = bf16[1040,512]{1,0:T(8,128)(2,1)S(1)} collective-permute-done((bf16[1040,512]{1,0:T(8,128)(2,1)S(1)}, bf16[1040,512]{1,0:T(8,128)(2,1)S(1)}, u32[]{:S(2)}, u32[]{:S(2)}) %collective-permute-start.1) | collective-permute-done | bytes 1064992 | tf_op jit(solution)/shard_map/ppermute | solution.py:432
  149.3 1.2 shard_map.150.mine_ref
  150.7 2.6 %collective-permute-done.2.other_ref = bf16[1040,512]{1,0:T(8,128)(2,1)S(1)} collective-permute-done((bf16[1040,512]{1,0:T(8,128)(2,1)S(1)}, bf16[1040,512]{1,0:T(8,128)(2,1)S(1)}, u32[]{:S(2)}, u32[]{:S(2)}) %collective-permute-start.2) | collective-permute-done | bytes 1064992 | tf_op jit(solution)/shard_map/ppermute | solution.py:432
  153.3 2.1 %shard_map.151.parts_ref = bf16[576,512]{1,0:T(8,128)(2,1)S(1)} custom-call(s32[1]{0:T(128)} %bitcast.place_ref, s32[1,512]{1,0:T(1,128)S(1)} %dynamic-slice_bitcast_fusion.3.pick_ref, bf16[1040,512]{1,0:T(8,128)(2,1)S(1)} %shard_map.150.mine_ref, bf16[1040,512]{1,0:T(8,128)(2,1)S(1)} %collective-permute-done.2.other_ref), custom_call_target="tpu_custom_call" | custom-call | flops 1000000000 | bytes 8388608 | tf_op jit(solution)/shard_map/pallas_call | solution.py:27
  155.4 0.8 copy-done.1
  156.2 35.6 %shard_map.152.level_ref = bf16[2048,512]{1,0:T(8,128)(2,1)} custom-call(bf16[576,512]{1,0:T(8,128)(2,1)} %copy-done.1, bf16[512,512]{1,0:T(8,128)(2,1)} %get-tuple-element.27.weight_ref), custom_call_target="tpu_custom_call" | custom-call | tf_op jit(solution)/shard_map/pallas_call | solution.py:544
  191.8 1.6 copy-done
  193.4 1.6 copy-done.13
  195.0 11.3 %shard_map.153 = bf16[2048,512]{1,0:T(8,128)(2,1)} custom-call(s32[1]{0:T(128)} %bitcast.place_ref, s32[1,2048]{1,0:T(1,128)S(1)} %get-tuple-element.18.two_ref, s32[1,2048]{1,0:T(1,128)S(1)} %get-tuple-element.19.three_ref, bf16[2048,512]{1,0:T(8,128)(2,1)S(1)} %copy-done.13, bf16[1040,512]{1,0:T(8,128)(2,1)S(1)} %shard_map.150.mine_ref, ...), custom_call_target="tpu_custom_call" | custom-call | flops 8589934592 | bytes 8388608 | tf_op jit(solution)/shard_map/pallas_call | solution.py:27
  (31 shorter events, 0.2 us)
Async XLA Ops:
  0.0 1.2 copy-start.2
  1.2 0.7 copy-start.8
  7.3 7.4 %copy-start.19 = (s32[1,1,16,2]{2,3,1,0:T(2,128)S(1)}, s32[1,1,16,2]{2,3,1,0:T(2,128)}, u32[]{:S(2)}) copy-start(s32[1,1,16,2]{2,3,1,0:T(2,128)} %param.17) | copy-start | bytes 388
  7.3 7.4 %copy-start.17 = (s32[1,1,2048,16]{2,3,1,0:T(8,128)S(1)}, s32[1,1,2048,16]{2,3,1,0:T(8,128)}, u32[]{:S(2)}) copy-start(s32[1,1,2048,16]{2,3,1,0:T(8,128)} %param.18) | copy-start | bytes 393220
  7.3 7.8 %copy-start.18 = (s32[2,1,2048]{2,1,0:T(1,128)S(1)}, s32[2,1,2048]{2,1,0:T(1,128)}, u32[]{:S(2)}) copy-start(s32[2,1,2048]{2,1,0:T(1,128)} %param.21) | copy-start | bytes 49156
  7.3 8.5 %copy-start.7 = (s32[1,1,2048]{2,1,0:T(1,128)S(1)}, s32[1,1,2048]{2,1,0:T(1,128)}, u32[]{:S(2)}) copy-start(s32[1,1,2048]{2,1,0:T(1,128)} %param.19) | copy-start | bytes 24580
  7.3 54.8 %all-to-all-start = ((bf16[32,64,512]{2,1,0:T(8,128)(2,1)}), bf16[32,64,512]{2,1,0:T(8,128)(2,1)S(1)}, u32[]{:S(2)}, u32[]{:S(2)}) async-start(bf16[32,64,512]{2,1,0:T(8,128)(2,1)} %bitcast.2), calls=%async_computation | async-start | bytes 4194304 | tf_op jit(solution)/shard_map/all_to_all | solution.py:468
  15.8 47.6 %copy-start.9 = (f32[512]{0:T(512)S(1)}, f32[512]{0:T(512)}, u32[]{:S(2)}) copy-start(f32[512]{0:T(512)} %param.23) | copy-start | bytes 6148
  15.9 47.6 %copy-start.10 = (f32[512]{0:T(512)S(1)}, f32[512]{0:T(512)}, u32[]{:S(2)}) copy-start(f32[512]{0:T(512)} %param.26) | copy-start | bytes 6148
  15.9 47.6 %copy-start.11 = (f32[512]{0:T(512)S(1)}, f32[512]{0:T(512)}, u32[]{:S(2)}) copy-start(f32[512]{0:T(512)} %param.28) | copy-start | bytes 6148
  62.2 1.3 copy-start.16
  63.5 1.2 copy-start.3
  64.7 1.2 copy-start.4
  66.0 1.0 copy-start.5
  67.0 1.0 copy-start.6
  107.7 1.3 copy-start.14
  109.0 4.9 %collective-permute-start = (bf16[2048,512]{1,0:T(8,128)(2,1)S(1)}, bf16[2048,512]{1,0:T(8,128)(2,1)}, u32[]{:S(2)}, u32[]{:S(2)}) collective-permute-start(bf16[2048,512]{1,0:T(8,128)(2,1)S(1)} %get-tuple-element.21.side_ref), channel_id=1, source_target_pairs={{0,4},{4,0},{8,12},{12,8},{16,20},{20,16},{24,28},{28,24},{1,5},{5... | collective-permute-start | bytes 6291464 | tf_op jit(solution)/shard_map/ppermute | solution.py:432
  113.9 11.3 %copy-start.15 = (bf16[2048,512]{1,0:T(8,128)(2,1)S(1)}, bf16[2048,512]{1,0:T(8,128)(2,1)}, u32[]{:S(2)}) copy-start(bf16[2048,512]{1,0:T(8,128)(2,1)} %copy-done.14) | copy-start | bytes 6291460
  123.0 26.3 %collective-permute-start.1 = (bf16[1040,512]{1,0:T(8,128)(2,1)S(1)}, bf16[1040,512]{1,0:T(8,128)(2,1)S(1)}, u32[]{:S(2)}, u32[]{:S(2)}) collective-permute-start(bf16[1040,512]{1,0:T(8,128)(2,1)S(1)} %get-tuple-element.22.mine_ref), channel_id=1, source_target_pairs={{0,8},{4,12},{8,0},{12,4},{16,24},{20,28},{24,16},{28,20},{1,9},{5... | collective-permute-start | bytes 3194888 | tf_op jit(solution)/shard_map/ppermute | solution.py:432
  131.1 19.4 %copy-start.12 = (bf16[2048,512]{1,0:T(8,128)(2,1)}, bf16[2048,512]{1,0:T(8,128)(2,1)S(1)}, u32[]{:S(2)}) copy-start(bf16[2048,512]{1,0:T(8,128)(2,1)S(1)} %shard_map.149.base_ref) | copy-start | bytes 6291460
  150.6 2.7 %collective-permute-start.2 = (bf16[1040,512]{1,0:T(8,128)(2,1)S(1)}, bf16[1040,512]{1,0:T(8,128)(2,1)S(1)}, u32[]{:S(2)}, u32[]{:S(2)}) collective-permute-start(bf16[1040,512]{1,0:T(8,128)(2,1)S(1)} %shard_map.150.mine_ref), channel_id=1, source_target_pairs={{0,4},{4,0},{8,12},{12,8},{16,20},{20,16},{24,28},{28,24},{1,5},{5... | collective-permute-start | bytes 3194888 | tf_op jit(solution)/shard_map/ppermute | solution.py:432
  155.4 0.8 copy-start.1
  191.8 1.6 copy-start
  193.4 1.6 copy-start.13
